TPU v7x, 512 devices: a whole 4x4x16 slice. The times are simulated.
512 devices in a mesh: mem: 32 (over z, core), lat: 16 (over x, y).
Axes of the slice: x: 4, y: 4, z: 16, core: 2. Of those that a mesh axis runs over, the one named last changes fastest.
Arguments:
- equivalents: float32 [384, 393216], P('mem', 'lat'), may hold values from -12 to 12
- innovations: float32 [384, 393216], P('mem', 'lat'), may hold values from -6 to 6
- obs_var: float32 [393216], P('lat'), may hold values from 0.5 to 2
- taper_tiles: bfloat16 [2, 512, 512], replicated, may hold values from 0 to 1
- region_blocks: int32 [16, 32], replicated, may hold values from 1 to 2, 48 in all within a row
- pair_mask: int32 [16, 48], replicated, may hold values 0 or 1
- taper_index: int32 [16, 48, 3], replicated, may hold values from 0 to 1
- eig_low: float32 [1], replicated, may hold values from 0.3 to 0.6
- eig_high: float32 [1], replicated, may hold values from 6 to 10
Outputs:
- solution: float32 [384, 393216], P('mem', 'lat')
Inputs may be any that keep to these rules, and one draw needn't show every extreme that they name: `region_blocks`: in every band the counts sum to 48 and some region holds exactly 2 blocks.
All inputs are finite; a program needn't handle non-finite values.
Results may differ from a plain program's by a relative error of at most 0.0044.
Values may be sent and summed in bfloat16 or wider, within the bound.
A program may use at most 64 MiB of HBM per device.

v0:
```python
import jax
import jax.numpy as jnp
from jax import lax
from jax.sharding import PartitionSpec as P

M = 384
BLOCK = 512
MAXB = 2
ITERS = 3


def extended(shard, sides, width):
    for axis, dim in sides:
        count, length = (lax.axis_size(axis), shard.shape[dim])
        up = [(i, (i + 1) % count) for i in range(count - 1)]
        down = [(j, i) for i, j in up]
        last = lax.slice_in_dim(shard, length - width, length, axis=dim)
        initial = lax.slice_in_dim(shard, 0, width, axis=dim)
        before = lax.ppermute(last, axis, up)
        after = lax.ppermute(initial, axis, down)
        shard = jnp.concatenate([before, shard, after], axis=dim)
    return shard


def block_prod(left_op, right_op, einsum_form):
    return jnp.einsum(einsum_form, left_op, right_op, preferred_element_type=jnp.float32)


def on_device(
    equivalents,
    innovations,
    obs_var,
    taper_tiles,
    region_blocks,
    pair_mask,
    taper_index,
    eig_low,
    eig_high,
):
    groups = lax.axis_size("mem")
    my_group = lax.axis_index("mem")
    my_band = lax.axis_index("lat")
    group_rows, band_cols = equivalents.shape
    band_count = band_cols // BLOCK
    inv_scale = (M - 1) ** (-0.5)
    starts_all = jnp.cumsum(region_blocks, axis=1) - region_blocks
    counts_band = lax.dynamic_index_in_dim(region_blocks, my_band, 0, keepdims=False)
    starts_band = lax.dynamic_index_in_dim(starts_all, my_band, 0, keepdims=False)
    slot_offsets = jnp.arange(MAXB, dtype=jnp.int32)
    slot_blocks = starts_band[:, None] + slot_offsets[None, :]
    slot_valid = (slot_offsets[None, :] < counts_band[:, None]).astype(jnp.float32)

    def pack_regions(values):
        blocks = jnp.swapaxes(values.reshape(group_rows, band_count, BLOCK), 0, 1)
        padded = jnp.concatenate(
            [blocks, jnp.zeros((MAXB, group_rows, BLOCK), values.dtype)], axis=0
        )
        picked = padded[slot_blocks] * slot_valid[:, :, None, None]
        return picked.reshape(groups * MAXB, group_rows, BLOCK)

    rhs_packed = pack_regions(innovations)
    raw_region, rhs_region = (
        lax.all_to_all(pack_regions(equivalents), "mem", split_axis=0, concat_axis=1, tiled=True),
        lax.all_to_all(rhs_packed, "mem", split_axis=0, concat_axis=1, tiled=True),
    )
    mean_rows = jnp.mean(raw_region, axis=1, keepdims=True)
    perturb = ((raw_region - mean_rows) * inv_scale).astype(jnp.bfloat16)
    region_start = starts_band[my_group]
    region_count = counts_band[my_group]
    own_valid = (slot_offsets < region_count).astype(jnp.float32)
    own_blocks = jnp.minimum(region_start + slot_offsets, band_count - 1)
    var_blocks = jnp.concatenate(
        [obs_var.reshape(band_count, BLOCK), jnp.zeros((MAXB, BLOCK), jnp.float32)], axis=0
    )
    variance = var_blocks[region_start + slot_offsets] * own_valid[:, None]
    index_band = lax.dynamic_index_in_dim(taper_index, my_band, 0, keepdims=False)
    mask_band = lax.dynamic_index_in_dim(pair_mask, my_band, 0, keepdims=False)
    taper_table = taper_tiles.astype(jnp.float32)
    own_index = index_band[own_blocks]
    tile_self = taper_table[own_index[:, 0]]
    tile_self = 0.5 * (tile_self + jnp.swapaxes(tile_self, 1, 2))
    cov_self = (tile_self * block_prod(perturb, perturb, "jmi,jmk->jik")).astype(jnp.bfloat16)
    east_active = (
        (slot_offsets[:-1] + 1 < region_count) & (mask_band[own_blocks[:-1]] == 1)
    ).astype(jnp.float32)
    tile_east = taper_table[own_index[:-1, 1]]
    cov_east = (
        tile_east
        * block_prod(perturb[:-1], perturb[1:], "jmi,jmk->jik")
        * east_active[:, None, None]
    ).astype(jnp.bfloat16)
    tile_north = taper_table[index_band[region_start, 2]]
    own_first = perturb[0]
    edge_rows = extended(perturb[0:1], (("lat", 0),), 1)
    cov_north = (tile_north * block_prod(own_first, edge_rows[2], "mi,mk->ik")).astype(jnp.bfloat16)
    lower_band = jnp.maximum(my_band - 1, 0)
    lower_start = starts_all[lower_band, my_group]
    tile_south = taper_table[taper_index[lower_band, lower_start, 2]]
    cov_south = (tile_south.T * block_prod(own_first, edge_rows[0], "mi,mk->ik")).astype(
        jnp.bfloat16
    )
    low_bound = eig_low[0]
    high_bound = eig_high[0]
    centre = 0.5 * (high_bound + low_bound)
    half_width = 0.5 * (high_bound - low_bound)
    ratio_scale = centre / half_width
    ratio_prev = 1.0 / ratio_scale
    residual = rhs_region
    solution = jnp.zeros_like(residual)
    direction = residual / centre
    for iteration in range(ITERS):
        solution = solution + direction
        if iteration + 1 < ITERS:
            dir_bf = direction.astype(jnp.bfloat16)
            edge_dirs = extended(dir_bf[0:1], (("lat", 0),), 1)
            result = variance[:, None, :] * direction + block_prod(cov_self, dir_bf, "jik,jmk->jmi")
            east_term = block_prod(cov_east, dir_bf[1:], "jik,jmk->jmi")
            west_term = block_prod(cov_east, dir_bf[:-1], "jki,jmk->jmi")
            zero_block = jnp.zeros((1, M, BLOCK), jnp.float32)
            edge_term = block_prod(cov_north, edge_dirs[2], "ik,mk->mi") + block_prod(
                cov_south, edge_dirs[0], "ik,mk->mi"
            )
            result = (
                result
                + jnp.concatenate([east_term, zero_block], axis=0)
                + jnp.concatenate([zero_block, west_term], axis=0)
            )
            residual = residual - (
                result
                + jnp.concatenate(
                    [edge_term[None], jnp.zeros((MAXB - 1, M, BLOCK), jnp.float32)], axis=0
                )
            )
            ratio_next = 1.0 / (2.0 * ratio_scale - ratio_prev)
            direction = (
                ratio_next * ratio_prev * direction + 2.0 * ratio_next / half_width * residual
            )
            ratio_prev = ratio_next
    returned = lax.all_to_all(solution, "mem", split_axis=1, concat_axis=0, tiled=True)
    block_ids = jnp.arange(band_count, dtype=jnp.int32)
    owners = jnp.sum((starts_band[None, :] <= block_ids[:, None]).astype(jnp.int32), axis=1) - 1
    source_slots = owners * MAXB + block_ids - starts_band[owners]
    picked = returned[source_slots]
    return jnp.swapaxes(picked, 0, 1).reshape(group_rows, band_cols)


def solution(mesh):
    return jax.shard_map(
        on_device,
        mesh=mesh,
        in_specs=(P("mem", "lat"), P("mem", "lat"), P("lat"), P(), P(), P(), P(), P(), P()),
        out_specs=P("mem", "lat"),
        check_vma=False,
    )
```

profile of v0, /device:TPU:1, one launch (start us, length us, event | category | flops | bytes accessed | tf_op | source)
XLA Modules:
  0.0 371.2 jit_solution(7244561087856695123)
XLA Ops:
  0.0 0.9 reduce_window_sum.11
  0.9 0.7 sub.46
  1.6 0.7 fusion.33
  2.5 2.3 copy.86
  4.9 0.7 copy.119
  5.6 0.7 copy-done.11
  6.3 0.9 copy.87
  7.4 0.7 copy.118
  8.5 2.1 gather_fusion
  10.6 2.0 gather_fusion.4
  12.8 3.9 %broadcast_multiply_fusion.1 = (f32[64,12,512]{2,1,0:T(8,128)}, f32[64,12,512]{2,1,0:T(8,128)S(1)}) fusion(f32[64,12,512]{2,1,0:T(8,128)} %gather_fusion, f32[64]{0:T(128)S(1)} %reshape.292, f32[64,12,512]{2,1,0:T(8,128)} %gather_fusion.4), kind=kLoop, calls=%fused_computation.38 | loop fusion | flops 786432 | bytes 6291712 | tf_op jit(solution)/shard_map/mul | solution.py:58
  16.7 117.3 %all_to_all.54 = f32[64,12,512]{2,1,0:T(8,128)} all-to-all(f32[64,12,512]{2,1,0:T(8,128)S(1)} %get-tuple-element.36), channel_id=1, replica_groups=mesh['mem'=32,'lat'=16] {'mem'}, dimensions={0} | all-to-all | bytes 3145728 | tf_op jit(solution)/shard_map/all_to_all | solution.py:63
  134.0 5.0 %all-to-all-start = ((f32[64,12,512]{2,1,0:T(8,128)}), f32[64,12,512]{2,1,0:T(8,128)}, u32[]{:S(2)}, u32[]{:S(2)}) async-start(f32[64,12,512]{2,1,0:T(8,128)} %get-tuple-element.35), calls=%async_computation | async-start | bytes 4194304 | tf_op jit(solution)/shard_map/all_to_all | solution.py:64
  139.0 1.3 dynamic_slice.41
  140.3 0.6 fusion.43
  144.7 1.4 constant_dynamic-slice_fusion.5
  150.2 0.7 constant_dynamic-slice_fusion.1
  151.3 0.8 fusion.30
  152.1 0.6 gather_fusion.2
  152.7 0.6 slice.36
  153.4 2.0 gather_fusion.3
  155.4 2.9 copy.67
  159.5 0.7 add_minimum_fusion
  160.3 1.3 dynamic-slice.10
  163.6 1.3 copy.73
  166.2 0.6 gather_fusion.1
  166.8 0.6 compare_convert_fusion
  167.4 3.1 bitcast_reduce_fusion
  170.5 0.9 fusion.4
  171.4 2.0 fusion.42
  173.5 1.3 collective-permute-start.1
  174.8 4.7 %collective-permute-start.3 = (bf16[1,384,512]{2,1,0:T(8,128)(2,1)S(1)}, bf16[1,384,512]{2,1,0:T(8,128)(2,1)}, u32[]{:S(2)}, u32[]{:S(2)}) collective-permute-start(bf16[1,384,512]{2,1,0:T(8,128)(2,1)S(1)} %copy.84), channel_id=1, source_target_pairs={{0,1},{1,2},{2,3},{3,4},{4,5},{5,6},{6,7},{7,8},{8,9},{9,10},{10,1... | collective-permute-start | bytes 1179656 | tf_op jit(solution)/shard_map/ppermute | solution.py:19
  179.5 58.5 %all-to-all-done = f32[64,12,512]{2,1,0:T(8,128)} async-done(((f32[64,12,512]{2,1,0:T(8,128)}), f32[64,12,512]{2,1,0:T(8,128)}, u32[]{:S(2)}, u32[]{:S(2)}) %all-to-all-start) | async-done | bytes 1572896 | tf_op jit(solution)/shard_map/all_to_all | solution.py:64
  238.0 3.0 copy.81
  241.3 3.5 collective-permute-start.2
  244.8 1.3 collective-permute-start
  246.1 0.8 fusion.2
  247.0 0.5 fusion.7
  247.5 0.4 convolution_bitcast_fusion.3
  248.2 0.4 copy-done.9
  248.7 1.5 fusion.11
  250.2 1.7 fusion.10
  251.8 0.4 fusion.23
  252.3 2.0 collective-permute-done
  254.3 0.4 fusion.9
  254.7 2.2 fusion.5
  256.9 3.2 collective-permute-start.5
  260.2 1.4 collective-permute-start.4
  261.7 0.4 convolution_bitcast_fusion.1
  262.1 0.4 convolution_bitcast_fusion
  262.4 2.4 collective-permute-done.5
  264.8 0.4 fusion.18
  265.2 3.6 collective-permute-done.4
  268.9 0.4 fusion.8
  269.3 1.3 add_add_fusion
  270.6 2.4 copy.76
  272.9 11.2 %all-to-all-start.2 = ((f32[2,384,512]{2,0,1:T(2,128)}), f32[2,384,512]{2,0,1:T(2,128)S(1)}, u32[]{:S(2)}, u32[]{:S(2)}) async-start(f32[2,384,512]{2,0,1:T(2,128)} %copy.76), calls=%async_computation.2 | async-start | bytes 3145728 | tf_op jit(solution)/shard_map/all_to_all | solution.py:139
  284.3 0.8 gather_fusion.5
  285.1 77.0 %all-to-all-done.2 = f32[2,384,512]{2,0,1:T(2,128)S(1)} async-done(((f32[2,384,512]{2,0,1:T(2,128)}), f32[2,384,512]{2,0,1:T(2,128)S(1)}, u32[]{:S(2)}, u32[]{:S(2)}) %all-to-all-start.2) | async-done | bytes 1572896 | tf_op jit(solution)/shard_map/all_to_all | solution.py:139
  362.1 1.1 copy-done.4
  363.2 1.8 copy.82
  365.0 1.8 gather_fusion.6
  366.8 2.1 copy.79
  369.1 2.1 copy.88
  (66 shorter events, 2.8 us)
Async XLA Ops:
  4.9 1.4 copy-start.11
  134.0 17.1 %copy-start.12 = (bf16[2,512,512]{2,1,0:T(8,128)(2,1)S(1)}, bf16[2,512,512]{2,1,0:T(8,128)(2,1)}, u32[]{:S(2)}) copy-start(bf16[2,512,512]{2,1,0:T(8,128)(2,1)} %param.12) | copy-start | bytes 3145732
  134.0 104.0 %all-to-all-start = ((f32[64,12,512]{2,1,0:T(8,128)}), f32[64,12,512]{2,1,0:T(8,128)}, u32[]{:S(2)}, u32[]{:S(2)}) async-start(f32[64,12,512]{2,1,0:T(8,128)} %get-tuple-element.35), calls=%async_computation | async-start | bytes 4194304 | tf_op jit(solution)/shard_map/all_to_all | solution.py:64
  163.6 1.3 copy-start.15
  173.5 76.7 %collective-permute-start.1 = (bf16[1,384,512]{2,1,0:T(8,128)(2,1)S(1)}, bf16[1,384,512]{2,1,0:T(8,128)(2,1)}, u32[]{:S(2)}, u32[]{:S(2)}) collective-permute-start(bf16[1,384,512]{2,1,0:T(8,128)(2,1)S(1)} %copy.84), channel_id=1, source_target_pairs={{1,0},{2,1},{3,2},{4,3},{5,4},{6,5},{7,6},{8,7},{9,8},{10,9},{11,1... | collective-permute-start | bytes 1179656 | tf_op jit(solution)/shard_map/ppermute | solution.py:20
  174.8 73.5 %collective-permute-start.3 = (bf16[1,384,512]{2,1,0:T(8,128)(2,1)S(1)}, bf16[1,384,512]{2,1,0:T(8,128)(2,1)}, u32[]{:S(2)}, u32[]{:S(2)}) collective-permute-start(bf16[1,384,512]{2,1,0:T(8,128)(2,1)S(1)} %copy.84), channel_id=1, source_target_pairs={{0,1},{1,2},{2,3},{3,4},{4,5},{5,6},{6,7},{7,8},{8,9},{9,10},{10,1... | collective-permute-start | bytes 1179656 | tf_op jit(solution)/shard_map/ppermute | solution.py:19
  238.0 8.1 %copy-start.1 = (f32[2,512,512]{1,2,0:T(8,128)S(1)}, f32[2,512,512]{1,2,0:T(8,128)}, u32[]{:S(2)}) copy-start(f32[2,512,512]{1,2,0:T(8,128)} %copy.67) | copy-start | bytes 6291460
  241.0 13.7 %copy-start.2 = (f32[32,2,12,512]{3,1,2,0:T(2,128)}, f32[32,2,12,512]{3,1,2,0:T(2,128)S(1)}, u32[]{:S(2)}) copy-start(f32[32,2,12,512]{3,1,2,0:T(2,128)S(1)} %copy.81) | copy-start | bytes 4718596
  241.0 5.1 %copy-start = (f32[2,512,512]{2,1,0:T(8,128)S(1)}, f32[2,512,512]{2,1,0:T(8,128)}, u32[]{:S(2)}) copy-start(f32[2,512,512]{2,1,0:T(8,128)} %gather_fusion.3) | copy-start | bytes 6291460
  241.3 5.7 %copy-start.10 = (bf16[1,384,512]{2,0,1:T(2,128)(2,1)S(1)}, bf16[1,384,512]{2,0,1:T(2,128)(2,1)}, u32[]{:S(2)}) copy-start(bf16[1,384,512]{2,0,1:T(2,128)(2,1)} %get-tuple-element.29) | copy-start | bytes 1179652
  241.3 10.5 %collective-permute-start.2 = (bf16[1,384,512]{2,1,0:T(8,128)(2,1)S(1)}, bf16[1,384,512]{2,1,0:T(8,128)(2,1)S(1)}, u32[]{:S(2)}, u32[]{:S(2)}) collective-permute-start(bf16[1,384,512]{2,1,0:T(8,128)(2,1)S(1)} %slice.75), channel_id=1, source_target_pairs={{0,1},{1,2},{2,3},{3,4},{4,5},{5,6},{6,7},{7,8},{8,9},{9,10},{10,1... | collective-permute-start | bytes 1179656 | tf_op jit(solution)/shard_map/ppermute | solution.py:19
  244.8 9.5 %collective-permute-start = (bf16[1,384,512]{2,1,0:T(8,128)(2,1)S(1)}, bf16[1,384,512]{2,1,0:T(8,128)(2,1)S(1)}, u32[]{:S(2)}, u32[]{:S(2)}) collective-permute-start(bf16[1,384,512]{2,1,0:T(8,128)(2,1)S(1)} %slice.75), channel_id=1, source_target_pairs={{1,0},{2,1},{3,2},{4,3},{5,4},{6,5},{7,6},{8,7},{9,8},{10,9},{11,1... | collective-permute-start | bytes 1179656 | tf_op jit(solution)/shard_map/ppermute | solution.py:20
  247.0 7.7 %copy-start.13 = (bf16[2,512,512]{2,1,0:T(8,128)(2,1)}, bf16[2,512,512]{2,1,0:T(8,128)(2,1)S(1)}, u32[]{:S(2)}) copy-start(bf16[2,512,512]{2,1,0:T(8,128)(2,1)S(1)} %fusion.2) | copy-start | bytes 3145732
  247.4 1.2 copy-start.9
  250.1 2.1 copy-start.7
  251.8 2.4 copy-start.5
  256.9 7.9 %collective-permute-start.5 = (bf16[1,384,512]{2,1,0:T(8,128)(2,1)S(1)}, bf16[1,384,512]{2,1,0:T(8,128)(2,1)S(1)}, u32[]{:S(2)}, u32[]{:S(2)}) collective-permute-start(bf16[1,384,512]{2,1,0:T(8,128)(2,1)S(1)} %slice.77), channel_id=1, source_target_pairs={{0,1},{1,2},{2,3},{3,4},{4,5},{5,6},{6,7},{7,8},{8,9},{9,10},{10,1... | collective-permute-start | bytes 1179656 | tf_op jit(solution)/shard_map/ppermute | solution.py:19
  260.2 4.6 %copy-start.8 = (bf16[512,512]{1,0:T(8,128)(2,1)S(1)}, bf16[512,512]{1,0:T(8,128)(2,1)}, u32[]{:S(2)}) copy-start(bf16[512,512]{1,0:T(8,128)(2,1)} %copy-done.7) | copy-start | bytes 1572868
  260.2 8.7 %collective-permute-start.4 = (bf16[1,384,512]{2,1,0:T(8,128)(2,1)S(1)}, bf16[1,384,512]{2,1,0:T(8,128)(2,1)S(1)}, u32[]{:S(2)}, u32[]{:S(2)}) collective-permute-start(bf16[1,384,512]{2,1,0:T(8,128)(2,1)S(1)} %slice.77), channel_id=1, source_target_pairs={{1,0},{2,1},{3,2},{4,3},{5,4},{6,5},{7,6},{8,7},{9,8},{10,9},{11,1... | collective-permute-start | bytes 1179656 | tf_op jit(solution)/shard_map/ppermute | solution.py:20
  262.1 6.8 %copy-start.6 = (bf16[512,512]{1,0:T(8,128)(2,1)S(1)}, bf16[512,512]{1,0:T(8,128)(2,1)}, u32[]{:S(2)}) copy-start(bf16[512,512]{1,0:T(8,128)(2,1)} %copy-done.5) | copy-start | bytes 1572868
  264.8 4.5 %copy-start.14 = (bf16[2,512,512]{2,1,0:T(8,128)(2,1)S(1)}, bf16[2,512,512]{2,1,0:T(8,128)(2,1)}, u32[]{:S(2)}) copy-start(bf16[2,512,512]{2,1,0:T(8,128)(2,1)} %copy-done.13) | copy-start | bytes 3145732
  264.8 4.5 %copy-start.16 = (f32[2,384,512]{2,1,0:T(8,128)S(1)}, f32[2,384,512]{2,1,0:T(8,128)}, u32[]{:S(2)}) copy-start(f32[2,384,512]{2,1,0:T(8,128)} %get-tuple-element.38) | copy-start | bytes 4718596
  265.2 4.1 %copy-start.3 = (f32[32,2,12,512]{3,1,2,0:T(2,128)S(1)}, f32[32,2,12,512]{3,1,2,0:T(2,128)}, u32[]{:S(2)}) copy-start(f32[32,2,12,512]{3,1,2,0:T(2,128)} %copy-done.2) | copy-start | bytes 4718596
  272.9 89.2 %all-to-all-start.2 = ((f32[2,384,512]{2,0,1:T(2,128)}), f32[2,384,512]{2,0,1:T(2,128)S(1)}, u32[]{:S(2)}, u32[]{:S(2)}) async-start(f32[2,384,512]{2,0,1:T(2,128)} %copy.76), calls=%async_computation.2 | async-start | bytes 3145728 | tf_op jit(solution)/shard_map/all_to_all | solution.py:139
  362.1 1.1 copy-start.4
where the time goes:
time: 374 us; the launch traced here: 371 us
  waiting for transfers between devices  144 us (39%)
  blocking collectives  117 us (31%)
  local copies, waits for them, and re-layouts  42.3 us (11%)
  starting transfers between devices  31.6 us (8%)
  between operations  12.9 us (3%)
  other arithmetic  12.5 us (3%)
  matrix products  11 us (3%)
    all_to_all x1, blocking collectives, on_device(): lax.all_to_all(pack_regions(equivalents), 'mem', split_axis=0, concat_axi...  117 us
    all_to_all x1, waiting for transfers between devices, on_device(): lax.all_to_all(solution, 'mem', split_axis=1, concat_axis=0, tiled=True)  77 us
    all_to_all x1, waiting for transfers between devices, on_device(): lax.all_to_all(rhs_packed, 'mem', split_axis=0, concat_axis=1, tiled=True)  58.5 us
    ppermute x3, starting transfers between devices, extended(): before = lax.ppermute(last, axis, up)  11.4 us
    all_to_all x1, starting transfers between devices, on_device(): lax.all_to_all(solution, 'mem', split_axis=1, concat_axis=0, tiled=True)  11.2 us
    dot_general x14, matrix products, block_prod(): jnp.einsum(einsum_form, left_op, right_op, preferred_element_type=jnp.flo...  11 us
    unnamed x39, local copies, waits for them, and re-layouts  7.88 us
  transfers between devices with their start and end apart: 8, of which 5 were waited for; matrix products, arithmetic and copies ran while one was open for 9% of the time, Pallas kernels for 0%

commit v1 on v0

v1 whole, which is shorter than its diff:
```python
import jax
import jax.numpy as jnp
from jax import lax
from jax.experimental import pallas as pl
from jax.experimental.pallas import tpu as pltpu
from jax.sharding import PartitionSpec as P

M = 384
BLOCK = 512
BAND = 48
GROUPS = 4
BF = jnp.bfloat16
F32 = jnp.float32
MESH = pl.DeviceIdType.MESH
VM = pl.BlockSpec(memory_space=pltpu.VMEM)
HB = pl.BlockSpec(memory_space=pl.ANY)
SM = pl.BlockSpec(memory_space=pltpu.SMEM)
INV = (M - 1) ** -0.5


def coefficients(lo, hi):
    low = jnp.full((1, BLOCK), lo, F32)
    high = jnp.full((1, BLOCK), hi, F32)
    centre = 0.5 * (high + low)
    half = 0.5 * (high - low)
    scale = centre / half
    q0 = 1.0 / scale
    q1 = 1.0 / (2.0 * scale - q0)
    q2 = 1.0 / (2.0 * scale - q1)
    return centre, q1 * q0, 2.0 * q1 / half, q2 * q1, 2.0 * q2 / half


def fill_starts(region_ref, band, starts):
    def step(m, total):
        starts[m] = total
        return total + region_ref[band, m]

    lax.fori_loop(0, 32, step, jnp.int32(0))


def peer_of(i, z, c):
    t = i // 2
    odd = t % 2
    dz = (8 - (t + 1) // 2) * (2 * odd - 1)
    return (z + dz + 16) % 16 * 2 + (c + 1 - i % 2) % 2


def mirror(i):
    t = i // 2
    return i + 4 * (t % 2) - 2


ROOT = 12.0**0.5


def pack_kernel(
    eq_hbm, inn_hbm, var_hbm, index_hbm, region_ref, mask_ref, lo_ref, hi_ref,
    send_p, send_low, send_r, var_out, pick,
    eq, inn, rows_here, rows_low, starts, low_starts, sem,
):
    me = lax.axis_index("mem")
    z, c = me // 2, me % 2
    band = lax.axis_index("lat")
    lower = (band + 15) % 16
    loads = [
        pltpu.make_async_copy(eq_hbm, eq, sem.at[0]),
        pltpu.make_async_copy(inn_hbm, inn, sem.at[1]),
        pltpu.make_async_copy(index_hbm.at[band], rows_here, sem.at[2]),
        pltpu.make_async_copy(index_hbm.at[lower], rows_low, sem.at[3]),
    ]
    for load in loads:
        load.start()
    fill_starts(region_ref, band, starts)
    fill_starts(region_ref, lower, low_starts)
    start = starts[me]
    second = jnp.minimum(start + 1, BAND - 1)
    var_loads = [
        pltpu.make_async_copy(var_hbm.at[block], var_out.at[n], sem.at[4 + n])
        for n, block in enumerate((start, second))
    ]
    for load in var_loads:
        load.start()

    def block_cols(i, slot):
        first = starts[peer_of(i, z, c)]
        return pl.ds(pl.multiple_of(jnp.minimum(first + slot, BAND - 1) * BLOCK, BLOCK), BLOCK)

    inv_centre = 1.0 / coefficients(lo_ref[0], hi_ref[0])[0]
    loads[0].wait()
    top = lax.broadcasted_iota(jnp.int32, (12, BLOCK), 0) == 0

    def pack_pert(i, carry):
        lows = []
        for slot in range(2):
            values = eq[:, block_cols(i, slot)]
            total = jnp.sum(values, axis=0, keepdims=True) * (1.0 / ROOT)
            shift = (total - values[0:1]) * (1.0 / (ROOT - 1.0))
            mixed = jnp.where(top, total, (values - shift) * INV).astype(BF)
            send_p[i, slot] = mixed.reshape(3, 4, BLOCK)
            low = total - total.astype(BF).astype(F32)
            lows += [low[:, 0:256], low[:, 256:512]]
        send_low[i] = jnp.concatenate(lows, axis=0).astype(BF)
        return carry

    lax.fori_loop(0, 32, pack_pert, 0)
    for load in loads[2:]:
        load.wait()
    one = lambda on: jnp.where(on, 1.0, 0.0).astype(F32)
    pick[0] = one(rows_here[start, 0] == 1)
    pick[1] = one(rows_here[second, 0] == 1)
    pick[2] = one(rows_here[start, 1] == 1)
    pick[3] = one(rows_here[start, 2] == 1)
    pick[4] = one(rows_low[low_starts[me], 2] == 1)
    pick[5] = one((region_ref[band, me] > 1) & (mask_ref[band, start] == 1))
    loads[1].wait()

    def pack_rhs(i, carry):
        for slot in range(2):
            values = inn[:, block_cols(i, slot)]
            send_r[i, slot] = (values * inv_centre).astype(BF).reshape(3, 4, BLOCK)
        return carry

    lax.fori_loop(0, 32, pack_rhs, 0)
    for load in var_loads:
        load.wait()


def pack(equivalents, innovations, variance, index, regions, mask, low, high):
    chunk = (3, 4, BLOCK)
    return pl.pallas_call(
        pack_kernel,
        out_shape=(
            jax.ShapeDtypeStruct((32, 2) + chunk, BF),
            jax.ShapeDtypeStruct((32, 4, 256), BF),
            jax.ShapeDtypeStruct((32, 2) + chunk, BF),
            jax.ShapeDtypeStruct((2, 1, BLOCK), F32),
            jax.ShapeDtypeStruct((8,), F32),
        ),
        in_specs=[HB, HB, HB, HB, SM, SM, SM, SM],
        out_specs=(VM, VM, VM, VM, SM),
        scratch_shapes=[
            pltpu.VMEM((12, BAND * BLOCK), F32),
            pltpu.VMEM((12, BAND * BLOCK), F32),
            pltpu.SMEM((BAND, 3), jnp.int32),
            pltpu.SMEM((BAND, 3), jnp.int32),
            pltpu.SMEM((32,), jnp.int32),
            pltpu.SMEM((32,), jnp.int32),
            pltpu.SemaphoreType.DMA((6,)),
        ],
        name="pack",
    )(equivalents, innovations, variance, index, regions, mask, low, high)


def exchange_kernel(
    send_p, send_low, send_r, var_ref, taper_ref, pick, lo_ref, hi_ref,
    out_ref,
    got_p, got_low, got_r, send_w, pert, pert_up, pert_down, sym, flip, mat_a, mat_b,
    dir0_up, dir0_down, dir1, dir1_up, dir1_down, kept,
    sem_send, sem_own, sem_p, sem_low, sem_r, sem_w, sem_lat, sem_pert, sem_d0, sem_d1,
):
    me = lax.axis_index("mem")
    z, c = me // 2, me % 2
    band = lax.axis_index("lat")
    upper = (band + 1) % 16
    lower = (band + 15) % 16
    barrier = pltpu.get_barrier_semaphore()

    def greet(i, carry):
        pl.semaphore_signal(barrier, inc=1, device_id={"mem": peer_of(i, z, c)}, device_id_type=MESH)
        return carry

    lax.fori_loop(0, 31, greet, 0)
    for other in (upper, lower):
        pl.semaphore_signal(barrier, inc=1, device_id={"lat": other}, device_id_type=MESH)

    centre, rho1, sig1, rho2, sig2 = coefficients(lo_ref[0], hi_ref[0])
    for n in range(2):
        tile = taper_ref[n].astype(F32)
        turned = tile.T
        sym[n] = 0.5 * (tile + turned)
        flip[n] = turned.astype(BF)

    pl.semaphore_wait(barrier, 33)

    def remote(src, dst, recv, i):
        return pltpu.make_async_remote_copy(
            src_ref=src, dst_ref=dst, send_sem=sem_send, recv_sem=recv,
            device_id={"mem": peer_of(i, z, c)}, device_id_type=MESH,
        )

    def spread(send, got, sems):
        for i in (0, 1):
            remote(send.at[i], got.at[i], sems.at[0], i).start()

        def one(i, carry):
            j = mirror(i)
            remote(send.at[i], got.at[j], sems.at[j // 8], i).start()
            return carry

        lax.fori_loop(2, 30, one, 0)
        remote(send.at[30], got.at[30], sems.at[3], 30).start()

    def arrived(got, sems, g):
        size = 8 if g < 3 else 7
        view = got.at[pl.ds(8 * g, size)]
        pltpu.make_async_copy(view, view, sems.at[g]).wait()

    spread(send_p, got_p, sem_p)
    spread(send_low, got_low, sem_low)
    spread(send_r, got_r, sem_r)
    own = [
        pltpu.make_async_copy(sent.at[31], got.at[31], sem_own.at[n])
        for n, (sent, got) in enumerate(
            ((send_p, got_p), (send_low, got_low), (send_r, got_r), (send_w, out_ref))
        )
    ]
    for copy in own[:3]:
        copy.start()

    for g in range(GROUPS):
        arrived(got_p, sem_p, g)
        arrived(got_low, sem_low, g)
    own[0].wait()
    own[1].wait()
    lows = got_low[...].reshape(128, 256)
    row = lax.broadcasted_iota(jnp.int32, (M, M), 0)
    col = lax.broadcasted_iota(jnp.int32, (M, M), 1)
    spot = row % 12 == 0
    centring = jnp.where(row == col, 1.0, 0.0) - 1.0 / 32.0
    centring = jnp.where(spot & (col % 12 == 0), centring, 0.0).astype(BF)
    wide_row = lax.broadcasted_iota(jnp.int32, (M, 128), 0)
    wide_col = lax.broadcasted_iota(jnp.int32, (M, 128), 1)
    part_of = jnp.where(wide_row == 12 * (wide_col // 4), 1.0, 0.0) - 1.0 / 32.0
    is_mean = lax.broadcasted_iota(jnp.int32, (M, BLOCK), 0) % 12 == 0
    for slot in range(2):
        raw = got_p[:, slot].reshape(M, BLOCK)
        halves = []
        for half in range(2):
            use = (wide_row % 12 == 0) & (wide_col % 4 == 2 * slot + half)
            weight = jnp.where(use, part_of, 0.0).astype(BF)
            halves.append(jnp.dot(weight, lows, preferred_element_type=F32))
        centred = jnp.dot(centring, raw, preferred_element_type=F32)
        centred = (centred + jnp.concatenate(halves, axis=1)) * INV
        pert[slot] = jnp.where(is_mean, centred, raw.astype(F32)).astype(BF)

    def to_lat(src, dst, recv, other):
        return pltpu.make_async_remote_copy(
            src_ref=src, dst_ref=dst, send_sem=sem_lat, recv_sem=recv,
            device_id={"lat": other}, device_id_type=MESH,
        )

    def to_both(src, dst_down, dst_up, sem_down, sem_up):
        to_lat(src, dst_down, sem_down, upper).start()
        to_lat(src, dst_up, sem_up, lower).start()

    def landed(view, sem):
        pltpu.make_async_copy(view, view, sem).wait()

    to_both(pert.at[0], pert_down, pert_up, sem_pert.at[0], sem_pert.at[1])
    north_on = jnp.where(band < 15, 1.0, 0.0).astype(F32)
    south_on = jnp.where(band > 0, 1.0, 0.0).astype(F32)

    def build(dst, base, left, right, tiles, which, on):
        def chunk(r, carry):
            rows = pl.ds(pl.multiple_of(r * 128, 128), 128)
            prod = lax.dot_general(
                left[:, rows], right[...], (((0,), (0,)), ((), ())), preferred_element_type=F32
            )
            share = pick[which]
            tile = tiles[1, rows].astype(F32) * share + tiles[0, rows].astype(F32) * (1.0 - share)
            value = tile * prod
            if on is not None:
                value = value * on
            dst[pl.ds(pl.multiple_of(base + r * 128, 128), 128)] = value.astype(BF)
            return carry

        lax.fori_loop(0, 4, chunk, 0)

    here0, here1 = pert.at[0], pert.at[1]
    build(mat_a, 0, here0, here0, sym, 0, None)
    build(mat_a, 512, here1, here0, flip, 2, pick[5])
    build(mat_b, 0, here0, here1, taper_ref, 2, pick[5])
    build(mat_b, 512, here1, here1, sym, 1, None)
    landed(pert_up, sem_pert.at[1])
    landed(pert_down, sem_pert.at[0])
    build(mat_a, 1024, pert_up, here0, flip, 3, north_on)
    build(mat_a, 1536, pert_down, here0, taper_ref, 4, south_on)

    var = (var_ref[0], var_ref[1])
    keep_d = [rho1 + sig1 * (centre - v) for v in var]
    keep_y = [(1.0 + rho2 - sig2 * v) * sig1 + sig2 for v in var]

    def times(parts, mat):
        total = None
        for n, part in enumerate(parts):
            prod = jnp.dot(part, mat[pl.ds(512 * n, 512)], preferred_element_type=F32)
            total = prod if total is None else total + prod
        return total

    def stage_a(g):
        arrived(got_r, sem_r, g)
        if g == 3:
            own[2].wait()
        rows = pl.ds(8 * g, 8)
        to_both(
            got_r.at[rows, 0], dir0_down.at[rows], dir0_up.at[rows],
            sem_d0.at[g, 0], sem_d0.at[g, 1],
        )

    def stage_b(g):
        rows = pl.ds(8 * g, 8)
        landed(dir0_up.at[rows], sem_d0.at[g, 1])
        landed(dir0_down.at[rows], sem_d0.at[g, 0])
        mine = [got_r[rows, s].reshape(96, BLOCK) for s in range(2)]
        above = dir0_up[rows].reshape(96, BLOCK)
        below = dir0_down[rows].reshape(96, BLOCK)
        prods = (times((mine[0], mine[1], above, below), mat_a), times(mine, mat_b))
        for s in range(2):
            dir1[g, s] = (keep_d[s] * mine[s].astype(F32) - sig1 * prods[s]).astype(BF)
            kept[g, s] = keep_y[s] * prods[s]
        to_both(
            dir1.at[g, 0], dir1_down.at[g], dir1_up.at[g], sem_d1.at[g, 0], sem_d1.at[g, 1]
        )

    def stage_c(g):
        landed(dir1_up.at[g], sem_d1.at[g, 1])
        landed(dir1_down.at[g], sem_d1.at[g, 0])
        mine = [dir1[g, s] for s in range(2)]
        prods = (
            times((mine[0], mine[1], dir1_up[g], dir1_down[g]), mat_a), times(mine, mat_b)
        )
        for s in range(2):
            total = (kept[g, s] + sig2 * prods[s]).astype(BF)
            send_w[pl.ds(8 * g, 8), s] = total.reshape(8, 3, 4, BLOCK)
        for i in range(8 * g, 8 * g + 8):
            if i == 31:
                continue
            j = i if i < 2 or i == 30 else mirror(i)
            remote(send_w.at[i], out_ref.at[j], sem_w, i).start()

    stage_a(0)
    stage_a(1)
    stage_b(0)
    stage_a(2)
    stage_b(1)
    stage_c(0)
    stage_a(3)
    stage_b(2)
    stage_c(1)
    stage_b(3)
    stage_c(2)
    stage_c(3)
    own[3].start()
    own[3].wait()

    most = pl.ds(0, 31)
    landed(out_ref.at[most], sem_w)
    for sent in (send_p, send_low, send_r, send_w):
        pltpu.make_async_copy(sent.at[most], sent.at[most], sem_send).wait()
    for _ in range(2):
        pltpu.make_async_copy(pert.at[0], pert.at[0], sem_lat).wait()
        pltpu.make_async_copy(dir0_up, dir0_up, sem_lat).wait()
        pltpu.make_async_copy(dir1_up, dir1_up, sem_lat).wait()


def exchange(send_p, send_low, send_r, variance, tapers, pick, low, high):
    chunk = (3, 4, BLOCK)
    dma = pltpu.SemaphoreType.DMA
    return pl.pallas_call(
        exchange_kernel,
        out_shape=jax.ShapeDtypeStruct((32, 2) + chunk, BF),
        in_specs=[VM, VM, VM, VM, VM, SM, SM, SM],
        out_specs=VM,
        scratch_shapes=[
            pltpu.VMEM((32, 2) + chunk, BF),
            pltpu.VMEM((32, 4, 256), BF),
            pltpu.VMEM((32, 2) + chunk, BF),
            pltpu.VMEM((32, 2) + chunk, BF),
            pltpu.VMEM((2, M, BLOCK), BF),
            pltpu.VMEM((M, BLOCK), BF),
            pltpu.VMEM((M, BLOCK), BF),
            pltpu.VMEM((2, BLOCK, BLOCK), F32),
            pltpu.VMEM((2, BLOCK, BLOCK), BF),
            pltpu.VMEM((4 * BLOCK, BLOCK), BF),
            pltpu.VMEM((2 * BLOCK, BLOCK), BF),
            pltpu.VMEM((32,) + chunk, BF),
            pltpu.VMEM((32,) + chunk, BF),
            pltpu.VMEM((GROUPS, 2, 96, BLOCK), BF),
            pltpu.VMEM((GROUPS, 96, BLOCK), BF),
            pltpu.VMEM((GROUPS, 96, BLOCK), BF),
            pltpu.VMEM((GROUPS, 2, 96, BLOCK), F32),
            dma,
            dma((4,)),
            dma((GROUPS,)),
            dma((GROUPS,)),
            dma((GROUPS,)),
            dma,
            dma,
            dma((2,)),
            dma((GROUPS, 2)),
            dma((GROUPS, 2)),
        ],
        compiler_params=pltpu.CompilerParams(
            collective_id=0, has_side_effects=True, vmem_limit_bytes=48 << 20
        ),
        name="exchange",
    )(send_p, send_low, send_r, variance, tapers, pick, low, high)


STEPS = 6
PER_STEP = BAND // STEPS


def finish_kernel(inn_ref, var_ref, got_ref, region_ref, lo_ref, hi_ref, out_ref, where):
    me = lax.axis_index("mem")
    z, c = me // 2, me % 2
    band = lax.axis_index("lat")
    step = pl.program_id(0)

    @pl.when(step == 0)
    def _():
        def one(m, total):
            dz = (m // 2 - z + 16) % 16
            t = jnp.where(dz < 8, 15 - 2 * dz, 2 * dz - 16)
            place = 2 * t + 1 - (m + c) % 2
            where[jnp.minimum(total + 1, BAND - 1)] = 2 * place + 1
            where[total] = 2 * place
            return total + region_ref[band, m]

        lax.fori_loop(0, 32, one, jnp.int32(0))

    centre, rho1, sig1, rho2, sig2 = coefficients(lo_ref[0], hi_ref[0])
    for n in range(PER_STEP):
        cols = pl.ds(n * BLOCK, BLOCK)
        var = var_ref[n]
        keep = rho1 + sig1 * (centre - var)
        factor = 1.0 + (1.0 + rho2 - sig2 * var) * keep + sig2 * (centre - var)
        entry = where[step * PER_STEP + n]
        local = (factor / centre) * inn_ref[:, cols]
        out_ref[:, cols] = local - got_ref[entry // 2, entry % 2].reshape(12, BLOCK).astype(F32)


def finish(innovations, variance, got, regions, low, high):
    width = PER_STEP * BLOCK
    return pl.pallas_call(
        finish_kernel,
        grid=(STEPS,),
        out_shape=jax.ShapeDtypeStruct((12, BAND * BLOCK), F32),
        in_specs=[
            pl.BlockSpec((12, width), lambda i: (0, i)),
            pl.BlockSpec((PER_STEP, 1, BLOCK), lambda i: (i, 0, 0)),
            VM, SM, SM, SM,
        ],
        out_specs=pl.BlockSpec((12, width), lambda i: (0, i)),
        scratch_shapes=[pltpu.SMEM((BAND,), jnp.int32)],
        name="finish",
    )(innovations, variance, got, regions, low, high)


def on_device(
    equivalents, innovations, obs_var, taper_tiles, region_blocks, pair_mask, taper_index,
    eig_low, eig_high,
):
    variance = obs_var.reshape(BAND, 1, BLOCK)
    send_p, send_low, send_r, own_var, pick = pack(
        equivalents, innovations, variance, taper_index, region_blocks, pair_mask, eig_low,
        eig_high,
    )
    got = exchange(send_p, send_low, send_r, own_var, taper_tiles, pick, eig_low, eig_high)
    return finish(innovations, variance, got, region_blocks, eig_low, eig_high)


def solution(mesh):
    return jax.shard_map(
        on_device,
        mesh=mesh,
        in_specs=(P("mem", "lat"), P("mem", "lat"), P("lat"), P(), P(), P(), P(), P(), P()),
        out_specs=P("mem", "lat"),
        check_vma=False,
    )
```

time: 374 us -> 149 us (0.40)
  waiting for transfers between devices: 144 us -> 0 us
  Pallas kernels: 0 us -> 140 us
  blocking collectives: 117 us -> 0 us
  local copies, waits for them, and re-layouts: 42.3 us -> 7.03 us
  starting transfers between devices: 31.6 us -> 0 us
  other arithmetic: 12.5 us -> 0 us
  between operations: 12.9 us -> 1.34 us
  matrix products: 11 us -> 0 us
    pallas_call x0 -> x3, Pallas kernels: none -> 140 us  [the longest x1 128 us: exchange(): pl.pallas_call(exchange_kernel, out_shape=jax.ShapeDtypeStruct((32, 2) +...]
    all_to_all x2 -> x0, waiting for transfers between devices: 136 us -> none  [the longest x1 77 us: on_device(): lax.all_to_all(solution, 'mem', split_axis=1, concat_axis=0, tiled=True)]
    all_to_all x1 -> x0, blocking collectives: 117 us -> none  [on_device(): lax.all_to_all(pack_regions(equivalents), 'mem', split_axis=0, concat_axi...]
    all_to_all x2 -> x0, starting transfers between devices: 16.2 us -> none  [the longest x1 11.2 us: on_device(): lax.all_to_all(solution, 'mem', split_axis=1, concat_axis=0, tiled=True)]
    ppermute x6 -> x0, starting transfers between devices: 15.4 us -> none  [the longest x3 11.4 us: extended(): before = lax.ppermute(last, axis, up)]
    gather x9 -> x0, local copies, waits for them, and re-layouts: 14.1 us -> none  [the longest x2 4.98 us: on_device(): tile_self = taper_table[own_index[:, 0]]]
    dot_general x14 -> x0, matrix products: 11 us -> none  [block_prod(): jnp.einsum(einsum_form, left_op, right_op, preferred_element_type=jnp.flo...]
    ppermute x6 -> x0, waiting for transfers between devices: 8.02 us -> none  [the longest x3 5.65 us: extended(): after = lax.ppermute(initial, axis, down)]
  transfers between devices with their start and end apart: 8 -> 0, of which waited for: 5 -> 0; matrix products, arithmetic and copies ran while one was open for 9% -> 0% of each run, Pallas kernels for 0% -> 0%
where the time goes in v1:
time: 149 us
  Pallas kernels  140 us (94%)
  local copies, waits for them, and re-layouts  7.03 us (5%)
    pallas_call x1, Pallas kernels, exchange(): pl.pallas_call(exchange_kernel, out_shape=jax.ShapeDtypeStruct((32, 2) +...  128 us
    unnamed x15, local copies, waits for them, and re-layouts  7.03 us
    pallas_call x1, Pallas kernels, pack(): pl.pallas_call(pack_kernel, out_shape=(jax.ShapeDtypeStruct((32, 2) + chu...  6.81 us
    pallas_call x1, Pallas kernels, finish(): pl.pallas_call(finish_kernel, grid=(STEPS,), out_shape=jax.ShapeDtypeStru...  5.73 us

profile of v1, /device:TPU:1, one launch (start us, length us, event | category | flops | bytes accessed | tf_op | source)
XLA Modules:
  0.0 148.9 jit_solution(16557473903926980888)
XLA Ops:
  1.3 1.7 %copy.10.index_hbm = s32[16,48,3]{2,1,0:T(8,128)} copy(s32[16,48,3]{1,0,2:T(8,128)} %param.15) | data formatting | bytes 18432 | tf_op args[6]
  3.0 0.0 copy-start.1
  3.0 6.8 %pack.1 = (bf16[32,2,3,4,512]{4,3,2,1,0:T(4,128)(2,1)}, bf16[32,4,256]{2,1,0:T(4,128)(2,1)}, bf16[32,2,3,4,512]{4,3,2,1,0:T(4,128)(2,1)}, f32[2,1,512]{2,1,0:T(1,128)}, f32[8]{0:T(128)}) custom-call(f32[12,24576]{1,0:T(8,128)} %eq_hbm.1, f32[12,24576]{1,0:T(8,128)} %inn_ref.1, f32[48,1,512]{2,1,0:T(1,128)} %bitcast.1, s32[16,48,3]{2,1,0:T(8,128)} %copy.10.index_hbm, ...), custom_call_target="tpu_custom_call" | custom-call | tf_op jit(solution)/shard_map/pack/pallas_call | solution.py:130
  9.8 0.0 copy-done.1
  9.8 0.0 copy-start.2
  9.8 1.1 copy-done.2
  11.0 0.0 copy-start.3
  11.0 1.1 copy-done.3
  12.1 0.0 copy-start.4
  12.1 0.8 copy-done.4
  12.9 0.0 copy-start.5
  13.0 0.7 copy-done.5
  13.6 0.0 copy-start.6
  13.6 0.7 copy-done.6
  14.3 128.0 %exchange.1.got_ref = bf16[32,2,3,4,512]{4,3,2,1,0:T(4,128)(2,1)S(1)} custom-call(bf16[32,2,3,4,512]{4,3,2,1,0:T(4,128)(2,1)S(1)} %copy-done.2, bf16[32,4,256]{2,1,0:T(4,128)(2,1)S(1)} %copy-done.4, bf16[32,2,3,4,512]{4,3,2,1,0:T(4,128)(2,1)S(1)} %copy-done.3, f32[2,1,512]{2,1,0:T(1,128)S(1)} %copy-done.5, bf16[2,512,512]{2,1,0:T(8,128)(2,1)S(1)} %copy-done.1, ...), custom_call_target="tpu_custom_call" | custom-call | tf_op jit(solution)/shard_map/exchange/pallas_call | solution.py:369
  142.3 0.0 copy-start
  142.3 0.9 copy-done
  143.1 5.7 %finish.1 = f32[12,24576]{1,0:T(8,128)} custom-call(f32[12,24576]{1,0:T(8,128)} %inn_ref.1, f32[48,1,512]{2,1,0:T(1,128)} %bitcast.2, bf16[32,2,3,4,512]{4,3,2,1,0:T(4,128)(2,1)} %copy-done, s32[16,32]{1,0:T(8,128)} %region_ref.3, f32[1]{0:T(128)S(6)} %copy.11.lo_ref, f32[1]{0:T(128)S(6)} %copy.12.hi_ref), custom_call_target="tpu_custom_call" | custom-call | tf_op jit(solution)/shard_map/finish/pallas_call | solution.py:445
Async XLA Ops:
  3.0 6.8 %copy-start.1 = (bf16[2,512,512]{2,1,0:T(8,128)(2,1)S(1)}, bf16[2,512,512]{2,1,0:T(8,128)(2,1)}, u32[]{:S(2)}) copy-start(bf16[2,512,512]{2,1,0:T(8,128)(2,1)} %taper_ref.1) | copy-start | bytes 3145732
  9.8 1.1 copy-start.2
  11.0 1.1 copy-start.3
  12.1 0.8 copy-start.4
  12.9 0.7 copy-start.5
  13.6 0.7 copy-start.6
  142.3 0.9 copy-start

commit v2 on v1

--- a/solution.py
+++ b/solution.py
@@ -9,6 +9,7 @@
 BLOCK = 512
 BAND = 48
 GROUPS = 4
+LIMIT = 60 * 1024 * 1024
 BF = jnp.bfloat16
 F32 = jnp.float32
 MESH = pl.DeviceIdType.MESH
@@ -30,14 +31,6 @@
     return centre, q1 * q0, 2.0 * q1 / half, q2 * q1, 2.0 * q2 / half
 
 
-def fill_starts(region_ref, band, starts):
-    def step(m, total):
-        starts[m] = total
-        return total + region_ref[band, m]
-
-    lax.fori_loop(0, 32, step, jnp.int32(0))
-
-
 def peer_of(i, z, c):
     t = i // 2
     odd = t % 2
@@ -53,41 +46,67 @@
 ROOT = 12.0**0.5
 
 
+CUTS = 6
+
+
 def pack_kernel(
-    eq_hbm, inn_hbm, var_hbm, index_hbm, region_ref, mask_ref, lo_ref, hi_ref,
-    send_p, send_low, send_r, var_out, pick,
-    eq, inn, rows_here, rows_low, starts, low_starts, sem,
+    eq_hbm, inn_hbm, var_hbm, index_ref, region_ref, mask_ref, lo_ref, hi_ref,
+    out_p, out_low, out_r, var_out, pick, where,
+    eq, inn, send_p, send_low, send_r, starts, low_starts, sem_eq, sem_inn, sem_var, sem_out,
 ):
     me = lax.axis_index("mem")
     z, c = me // 2, me % 2
     band = lax.axis_index("lat")
     lower = (band + 15) % 16
-    loads = [
-        pltpu.make_async_copy(eq_hbm, eq, sem.at[0]),
-        pltpu.make_async_copy(inn_hbm, inn, sem.at[1]),
-        pltpu.make_async_copy(index_hbm.at[band], rows_here, sem.at[2]),
-        pltpu.make_async_copy(index_hbm.at[lower], rows_low, sem.at[3]),
-    ]
-    for load in loads:
-        load.start()
-    fill_starts(region_ref, band, starts)
-    fill_starts(region_ref, lower, low_starts)
+    loads = []
+    for source, target, sems in ((eq_hbm, eq, sem_eq), (inn_hbm, inn, sem_inn)):
+        for n in range(CUTS):
+            cols = pl.ds(n * (BAND * BLOCK // CUTS), BAND * BLOCK // CUTS)
+            load = pltpu.make_async_copy(source.at[:, cols], target.at[:, cols], sems.at[n])
+            load.start()
+            loads.append(load)
+
+    def scan(m, totals):
+        total, low_total = totals
+        starts[m] = total
+        low_starts[m] = low_total
+        dz = (m // 2 - z + 16) % 16
+        t = jnp.where(dz < 8, 15 - 2 * dz, 2 * dz - 16)
+        place = 2 * t + 1 - (m + c) % 2
+        where[jnp.minimum(total + 1, BAND - 1)] = 2 * place + 1
+        where[total] = 2 * place
+        return total + region_ref[band, m], low_total + region_ref[lower, m]
+
+    lax.fori_loop(0, 32, scan, (jnp.int32(0), jnp.int32(0)))
     start = starts[me]
     second = jnp.minimum(start + 1, BAND - 1)
     var_loads = [
-        pltpu.make_async_copy(var_hbm.at[block], var_out.at[n], sem.at[4 + n])
+        pltpu.make_async_copy(var_hbm.at[block], var_out.at[n], sem_var.at[n])
         for n, block in enumerate((start, second))
     ]
     for load in var_loads:
         load.start()
 
+    def one(on):
+        return jnp.where(on, 1.0, 0.0).astype(F32)
+
+    pick[0] = one(index_ref[0, band, start] == 1)
+    pick[1] = one(index_ref[0, band, second] == 1)
+    pick[2] = one(index_ref[1, band, start] == 1)
+    pick[3] = one(index_ref[2, band, start] == 1)
+    pick[4] = one(index_ref[2, lower, low_starts[me]] == 1)
+    pick[5] = one((region_ref[band, me] > 1) & (mask_ref[band, start] == 1))
+    pick[6] = one(band < 15)
+    pick[7] = one(band > 0)
+
     def block_cols(i, slot):
         first = starts[peer_of(i, z, c)]
         return pl.ds(pl.multiple_of(jnp.minimum(first + slot, BAND - 1) * BLOCK, BLOCK), BLOCK)
 
     inv_centre = 1.0 / coefficients(lo_ref[0], hi_ref[0])[0]
-    loads[0].wait()
     top = lax.broadcasted_iota(jnp.int32, (12, BLOCK), 0) == 0
+    for load in loads[:CUTS]:
+        load.wait()
 
     def pack_pert(i, carry):
         lows = []
@@ -102,17 +121,16 @@
         send_low[i] = jnp.concatenate(lows, axis=0).astype(BF)
         return carry
 
-    lax.fori_loop(0, 32, pack_pert, 0)
-    for load in loads[2:]:
+    lax.fori_loop(0, 32, pack_pert, 0, unroll=2)
+    stores = [
+        pltpu.make_async_copy(send_p, out_p, sem_out.at[0]),
+        pltpu.make_async_copy(send_low, out_low, sem_out.at[1]),
+        pltpu.make_async_copy(send_r, out_r, sem_out.at[2]),
+    ]
+    stores[0].start()
+    stores[1].start()
+    for load in loads[CUTS:]:
         load.wait()
-    one = lambda on: jnp.where(on, 1.0, 0.0).astype(F32)
-    pick[0] = one(rows_here[start, 0] == 1)
-    pick[1] = one(rows_here[second, 0] == 1)
-    pick[2] = one(rows_here[start, 1] == 1)
-    pick[3] = one(rows_here[start, 2] == 1)
-    pick[4] = one(rows_low[low_starts[me], 2] == 1)
-    pick[5] = one((region_ref[band, me] > 1) & (mask_ref[band, start] == 1))
-    loads[1].wait()
 
     def pack_rhs(i, carry):
         for slot in range(2):
@@ -120,40 +138,50 @@
             send_r[i, slot] = (values * inv_centre).astype(BF).reshape(3, 4, BLOCK)
         return carry
 
-    lax.fori_loop(0, 32, pack_rhs, 0)
-    for load in var_loads:
-        load.wait()
+    lax.fori_loop(0, 32, pack_rhs, 0, unroll=4)
+    stores[2].start()
+    for copy in var_loads + stores:
+        copy.wait()
 
 
 def pack(equivalents, innovations, variance, index, regions, mask, low, high):
-    chunk = (3, 4, BLOCK)
+    chunks = (32, 2, 3, 4, BLOCK)
+    lows = (32, 4, 256)
+    dma = pltpu.SemaphoreType.DMA
     return pl.pallas_call(
         pack_kernel,
         out_shape=(
-            jax.ShapeDtypeStruct((32, 2) + chunk, BF),
-            jax.ShapeDtypeStruct((32, 4, 256), BF),
-            jax.ShapeDtypeStruct((32, 2) + chunk, BF),
+            jax.ShapeDtypeStruct(chunks, BF),
+            jax.ShapeDtypeStruct(lows, BF),
+            jax.ShapeDtypeStruct(chunks, BF),
             jax.ShapeDtypeStruct((2, 1, BLOCK), F32),
             jax.ShapeDtypeStruct((8,), F32),
+            jax.ShapeDtypeStruct((BAND,), jnp.int32),
         ),
-        in_specs=[HB, HB, HB, HB, SM, SM, SM, SM],
-        out_specs=(VM, VM, VM, VM, SM),
+        in_specs=[HB, HB, HB, SM, SM, SM, SM, SM],
+        out_specs=(HB, HB, HB, VM, SM, SM),
         scratch_shapes=[
             pltpu.VMEM((12, BAND * BLOCK), F32),
             pltpu.VMEM((12, BAND * BLOCK), F32),
-            pltpu.SMEM((BAND, 3), jnp.int32),
-            pltpu.SMEM((BAND, 3), jnp.int32),
+            pltpu.VMEM(chunks, BF),
+            pltpu.VMEM(lows, BF),
+            pltpu.VMEM(chunks, BF),
             pltpu.SMEM((32,), jnp.int32),
             pltpu.SMEM((32,), jnp.int32),
-            pltpu.SemaphoreType.DMA((6,)),
+            dma((CUTS,)),
+            dma((CUTS,)),
+            dma((2,)),
+            dma((3,)),
         ],
+        compiler_params=pltpu.CompilerParams(vmem_limit_bytes=LIMIT),
         name="pack",
     )(equivalents, innovations, variance, index, regions, mask, low, high)
 
 
 def exchange_kernel(
-    send_p, send_low, send_r, var_ref, taper_ref, pick, lo_ref, hi_ref,
+    send_p, send_low, send_r, var_hbm, taper_hbm, pick, lo_ref, hi_ref,
     out_ref,
+    var_ref, taper_ref,
     got_p, got_low, got_r, send_w, pert, pert_up, pert_down, sym, flip, mat_a, mat_b,
     dir0_up, dir0_down, dir1, dir1_up, dir1_down, kept,
     sem_send, sem_own, sem_p, sem_low, sem_r, sem_w, sem_lat, sem_pert, sem_d0, sem_d1,
@@ -163,6 +191,12 @@
     band = lax.axis_index("lat")
     upper = (band + 1) % 16
     lower = (band + 15) % 16
+    fetches = [
+        pltpu.make_async_copy(taper_hbm, taper_ref, sem_own.at[4]),
+        pltpu.make_async_copy(var_hbm, var_ref, sem_own.at[5]),
+    ]
+    for fetch in fetches:
+        fetch.start()
     barrier = pltpu.get_barrier_semaphore()
 
     def greet(i, carry):
@@ -174,6 +208,8 @@
         pl.semaphore_signal(barrier, inc=1, device_id={"lat": other}, device_id_type=MESH)
 
     centre, rho1, sig1, rho2, sig2 = coefficients(lo_ref[0], hi_ref[0])
+    for fetch in fetches:
+        fetch.wait()
     for n in range(2):
         tile = taper_ref[n].astype(F32)
         turned = tile.T
@@ -257,8 +293,8 @@
         pltpu.make_async_copy(view, view, sem).wait()
 
     to_both(pert.at[0], pert_down, pert_up, sem_pert.at[0], sem_pert.at[1])
-    north_on = jnp.where(band < 15, 1.0, 0.0).astype(F32)
-    south_on = jnp.where(band > 0, 1.0, 0.0).astype(F32)
+    north_on = pick[6]
+    south_on = pick[7]
 
     def build(dst, base, left, right, tiles, which, on):
         def chunk(r, carry):
@@ -369,9 +405,11 @@
     return pl.pallas_call(
         exchange_kernel,
         out_shape=jax.ShapeDtypeStruct((32, 2) + chunk, BF),
-        in_specs=[VM, VM, VM, VM, VM, SM, SM, SM],
-        out_specs=VM,
+        in_specs=[HB, HB, HB, HB, HB, SM, SM, SM],
+        out_specs=HB,
         scratch_shapes=[
+            pltpu.VMEM((2, 1, BLOCK), F32),
+            pltpu.VMEM((2, BLOCK, BLOCK), BF),
             pltpu.VMEM((32, 2) + chunk, BF),
             pltpu.VMEM((32, 4, 256), BF),
             pltpu.VMEM((32, 2) + chunk, BF),
@@ -390,7 +428,7 @@
             pltpu.VMEM((GROUPS, 96, BLOCK), BF),
             pltpu.VMEM((GROUPS, 2, 96, BLOCK), F32),
             dma,
-            dma((4,)),
+            dma((6,)),
             dma((GROUPS,)),
             dma((GROUPS,)),
             dma((GROUPS,)),
@@ -401,46 +439,31 @@
             dma((GROUPS, 2)),
         ],
         compiler_params=pltpu.CompilerParams(
-            collective_id=0, has_side_effects=True, vmem_limit_bytes=48 << 20
+            collective_id=0, has_side_effects=True, vmem_limit_bytes=LIMIT
         ),
         name="exchange",
     )(send_p, send_low, send_r, variance, tapers, pick, low, high)
 
 
-STEPS = 6
+STEPS = 4
 PER_STEP = BAND // STEPS
 
 
-def finish_kernel(inn_ref, var_ref, got_ref, region_ref, lo_ref, hi_ref, out_ref, where):
-    me = lax.axis_index("mem")
-    z, c = me // 2, me % 2
-    band = lax.axis_index("lat")
+def finish_kernel(inn_ref, var_ref, got_ref, where, lo_ref, hi_ref, out_ref):
     step = pl.program_id(0)
-
-    @pl.when(step == 0)
-    def _():
-        def one(m, total):
-            dz = (m // 2 - z + 16) % 16
-            t = jnp.where(dz < 8, 15 - 2 * dz, 2 * dz - 16)
-            place = 2 * t + 1 - (m + c) % 2
-            where[jnp.minimum(total + 1, BAND - 1)] = 2 * place + 1
-            where[total] = 2 * place
-            return total + region_ref[band, m]
-
-        lax.fori_loop(0, 32, one, jnp.int32(0))
-
     centre, rho1, sig1, rho2, sig2 = coefficients(lo_ref[0], hi_ref[0])
+    inv_centre = 1.0 / centre
     for n in range(PER_STEP):
         cols = pl.ds(n * BLOCK, BLOCK)
         var = var_ref[n]
         keep = rho1 + sig1 * (centre - var)
         factor = 1.0 + (1.0 + rho2 - sig2 * var) * keep + sig2 * (centre - var)
         entry = where[step * PER_STEP + n]
-        local = (factor / centre) * inn_ref[:, cols]
+        local = (factor * inv_centre) * inn_ref[:, cols]
         out_ref[:, cols] = local - got_ref[entry // 2, entry % 2].reshape(12, BLOCK).astype(F32)
 
 
-def finish(innovations, variance, got, regions, low, high):
+def finish(innovations, variance, got, where, low, high):
     width = PER_STEP * BLOCK
     return pl.pallas_call(
         finish_kernel,
@@ -452,9 +475,8 @@
             VM, SM, SM, SM,
         ],
         out_specs=pl.BlockSpec((12, width), lambda i: (0, i)),
-        scratch_shapes=[pltpu.SMEM((BAND,), jnp.int32)],
         name="finish",
-    )(innovations, variance, got, regions, low, high)
+    )(innovations, variance, got, where, low, high)
 
 
 def on_device(
@@ -462,12 +484,12 @@
     eig_low, eig_high,
 ):
     variance = obs_var.reshape(BAND, 1, BLOCK)
-    send_p, send_low, send_r, own_var, pick = pack(
-        equivalents, innovations, variance, taper_index, region_blocks, pair_mask, eig_low,
+    send_p, send_low, send_r, own_var, pick, where = pack(
+        equivalents, innovations, variance, jnp.transpose(taper_index, (2, 0, 1)), region_blocks, pair_mask, eig_low,
         eig_high,
     )
     got = exchange(send_p, send_low, send_r, own_var, taper_tiles, pick, eig_low, eig_high)
-    return finish(innovations, variance, got, region_blocks, eig_low, eig_high)
+    return finish(innovations, variance, got, where, eig_low, eig_high)
 
 
 def solution(mesh):

time: 149 us -> 141 us (0.946)
  local copies, waits for them, and re-layouts: 7.03 us -> 0 us
    unnamed x15 -> x0, local copies, waits for them, and re-layouts: 7.03 us -> none
    pallas_call x1, Pallas kernels: 5.73 us -> 4.05 us  [finish(): pl.pallas_call(finish_kernel, grid=(STEPS,), out_shape=jax.ShapeDtypeStru...]
where the time goes in v2:
time: 141 us
  Pallas kernels  139 us (99%)
    pallas_call x1, Pallas kernels, exchange(): pl.pallas_call(exchange_kernel, out_shape=jax.ShapeDtypeStruct((32, 2) +...  128 us
    pallas_call x1, Pallas kernels, pack(): pl.pallas_call(pack_kernel, out_shape=(jax.ShapeDtypeStruct(chunks, BF),...  6.94 us
    pallas_call x1, Pallas kernels, finish(): pl.pallas_call(finish_kernel, grid=(STEPS,), out_shape=jax.ShapeDtypeStru...  4.05 us

profile of v2, /device:TPU:1, one launch (start us, length us, event | category | flops | bytes accessed | tf_op | source)
XLA Modules:
  0.0 140.7 jit_solution(12944644317768351671)
XLA Ops:
  1.3 6.9 %pack.1 = (bf16[32,2,3,4,512]{4,3,2,1,0:T(4,128)(2,1)}, bf16[32,4,256]{2,1,0:T(4,128)(2,1)}, bf16[32,2,3,4,512]{4,3,2,1,0:T(4,128)(2,1)}, f32[2,1,512]{2,1,0:T(1,128)}, f32[8]{0:T(128)}, /*index=5*/s32[48]{0:T(128)}) custom-call(f32[12,24576]{1,0:T(8,128)} %eq_hbm.1, f32[12,24576]{1,0:T(8,128)} %inn_ref.1, f32[48,1,512]{2,1,0:T(1,128)} %bitcast.2, ...), custom_call_target="tpu_custom_call" | custom-call | tf_op jit(solution)/shard_map/pack/pallas_call | solution.py:151
  8.2 128.4 %exchange.1.got_ref = bf16[32,2,3,4,512]{4,3,2,1,0:T(4,128)(2,1)} custom-call(bf16[32,2,3,4,512]{4,3,2,1,0:T(4,128)(2,1)} %get-tuple-element.11.send_p, bf16[32,4,256]{2,1,0:T(4,128)(2,1)} %get-tuple-element.12.send_low, bf16[32,2,3,4,512]{4,3,2,1,0:T(4,128)(2,1)} %get-tuple-element.13.send_r, f32[2,1,512]{2,1,0:T(1,128)} %get-tuple-element.14.var_hbm, ...), custom_call_target="tpu_custom_call" | custom-call | tf_op jit(solution)/shard_map/exchange/pallas_call | solution.py:405
  136.7 4.0 %finish.1 = f32[12,24576]{1,0:T(8,128)} custom-call(f32[12,24576]{1,0:T(8,128)} %inn_ref.1, f32[48,1,512]{2,1,0:T(1,128)} %bitcast.3, bf16[32,2,3,4,512]{4,3,2,1,0:T(4,128)(2,1)} %exchange.1.got_ref, s32[48]{0:T(128)} %get-tuple-element.16.where, f32[1]{0:T(128)S(6)} %copy.10.lo_ref, f32[1]{0:T(128)S(6)} %copy.11.hi_ref), custom_call_target="tpu_custom_call" | custom-call | tf_op jit(solution)/shard_map/finish/pallas_call | solution.py:468

commit v3 on v2

v3 whole, which is shorter than its diff:
```python
import jax
import jax.numpy as jnp
from jax import lax
from jax.experimental import pallas as pl
from jax.experimental.pallas import tpu as pltpu
from jax.sharding import PartitionSpec as P

M = 384
BLOCK = 512
BAND = 48
GROUPS = 4
LIMIT = 60 * 1024 * 1024
BF = jnp.bfloat16
F32 = jnp.float32
MESH = pl.DeviceIdType.MESH
VM = pl.BlockSpec(memory_space=pltpu.VMEM)
HB = pl.BlockSpec(memory_space=pl.ANY)
SM = pl.BlockSpec(memory_space=pltpu.SMEM)
INV = (M - 1) ** -0.5


def coefficients(lo, hi):
    low = jnp.full((1, BLOCK), lo, F32)
    high = jnp.full((1, BLOCK), hi, F32)
    centre = 0.5 * (high + low)
    half = 0.5 * (high - low)
    scale = centre / half
    q0 = 1.0 / scale
    q1 = 1.0 / (2.0 * scale - q0)
    q2 = 1.0 / (2.0 * scale - q1)
    return centre, q1 * q0, 2.0 * q1 / half, q2 * q1, 2.0 * q2 / half


def peer_of(i, z, c):
    t = i // 2
    odd = t % 2
    dz = (8 - (t + 1) // 2) * (2 * odd - 1)
    return (z + dz + 16) % 16 * 2 + (c + 1 - i % 2) % 2


def mirror(i):
    t = i // 2
    return i + 4 * (t % 2) - 2


ROOT = 12.0**0.5


def tables_kernel(index_ref, region_ref, mask_ref, blocks, pick, where, starts, low_starts):
    me = lax.axis_index("mem")
    z, c = me // 2, me % 2
    band = lax.axis_index("lat")
    lower = (band + 15) % 16

    def scan(m, totals):
        total, low_total = totals
        starts[m] = total
        low_starts[m] = low_total
        dz = (m // 2 - z + 16) % 16
        t = jnp.where(dz < 8, 15 - 2 * dz, 2 * dz - 16)
        place = 2 * (2 * t + 1 - (m + c) % 2)
        follow = jnp.minimum(total + 1, BAND - 1)
        where[follow] = place + 1
        where[total] = place
        blocks[place] = total
        blocks[place + 1] = follow
        return total + region_ref[band, m], low_total + region_ref[lower, m]

    lax.fori_loop(0, 32, scan, (jnp.int32(0), jnp.int32(0)), unroll=4)
    start = starts[me]
    second = jnp.minimum(start + 1, BAND - 1)

    def one(on):
        return jnp.where(on, 1.0, 0.0).astype(F32)

    pick[0] = one(index_ref[0, band, start] == 1)
    pick[1] = one(index_ref[0, band, second] == 1)
    pick[2] = one(index_ref[1, band, start] == 1)
    pick[3] = one(index_ref[2, band, start] == 1)
    pick[4] = one(index_ref[2, lower, low_starts[me]] == 1)
    pick[5] = one((region_ref[band, me] > 1) & (mask_ref[band, start] == 1))
    pick[6] = one(band < 15)
    pick[7] = one(band > 0)


def tables(index, regions, mask):
    return pl.pallas_call(
        tables_kernel,
        out_shape=(
            jax.ShapeDtypeStruct((64,), jnp.int32),
            jax.ShapeDtypeStruct((8,), F32),
            jax.ShapeDtypeStruct((BAND,), jnp.int32),
        ),
        in_specs=[SM, SM, SM],
        out_specs=(SM, SM, SM),
        scratch_shapes=[pltpu.SMEM((32,), jnp.int32), pltpu.SMEM((32,), jnp.int32)],
        name="tables",
    )(index, regions, mask)


def exchange_kernel(
    eq_hbm, inn_hbm, var_hbm, taper_hbm, blocks, pick, lo_ref, hi_ref,
    out_ref, base_hbm,
    base_ref,
    eq, inn, var_ref, taper_ref, send_p, send_low, send_r,
    got_p, got_low, got_r, send_w, pert, pert_up, pert_down, sym, flip, mat_a, mat_b,
    dir0_up, dir0_down, dir1, dir1_up, dir1_down, kept,
    sem_send, sem_own, sem_in, sem_p, sem_low, sem_r, sem_w, sem_lat, sem_pert, sem_d0, sem_d1,
):
    me = lax.axis_index("mem")
    z, c = me // 2, me % 2
    band = lax.axis_index("lat")
    upper = (band + 1) % 16
    lower = (band + 15) % 16

    def column(k):
        return pl.ds(pl.multiple_of(k * BLOCK, BLOCK), BLOCK)

    def fetch_block(source, target, n, k):
        return pltpu.make_async_copy(source.at[:, column(k)], target.at[k], sem_in.at[n, k])

    def start_fetch(source, target, n):
        def one(k, carry):
            fetch_block(source, target, n, k).start()
            return carry

        lax.fori_loop(0, BAND, one, 0)

    def end_fetch(source, target, n):
        def one(k, carry):
            fetch_block(source, target, n, k).wait()
            return carry

        lax.fori_loop(0, BAND, one, 0)

    barrier = pltpu.get_barrier_semaphore()

    def greet(i, carry):
        pl.semaphore_signal(barrier, inc=1, device_id={"mem": peer_of(i, z, c)}, device_id_type=MESH)
        return carry

    lax.fori_loop(0, 31, greet, 0)
    for other in (upper, lower):
        pl.semaphore_signal(barrier, inc=1, device_id={"lat": other}, device_id_type=MESH)

    centre, rho1, sig1, rho2, sig2 = coefficients(lo_ref[0], hi_ref[0])
    start_fetch(eq_hbm, eq, 0)
    start_fetch(inn_hbm, inn, 1)
    fetches = [
        pltpu.make_async_copy(taper_hbm, taper_ref, sem_own.at[4]),
        pltpu.make_async_copy(var_hbm, var_ref, sem_own.at[5]),
    ]
    for fetch in fetches:
        fetch.start()
    top = lax.broadcasted_iota(jnp.int32, (12, BLOCK), 0) == 0
    end_fetch(eq_hbm, eq, 0)

    def pack_pert(i, carry):
        lows = []
        for slot in range(2):
            values = eq[blocks[2 * i + slot]]
            total = jnp.sum(values, axis=0, keepdims=True) * (1.0 / ROOT)
            shift = (total - values[0:1]) * (1.0 / (ROOT - 1.0))
            mixed = jnp.where(top, total, (values - shift) * INV).astype(BF)
            send_p[i, slot] = mixed.reshape(3, 4, BLOCK)
            low = total - total.astype(BF).astype(F32)
            lows += [low[:, 0:256], low[:, 256:512]]
        send_low[i] = jnp.concatenate(lows, axis=0).astype(BF)
        return carry

    lax.fori_loop(0, 32, pack_pert, 0, unroll=2)
    pl.semaphore_wait(barrier, 33)

    def remote(src, dst, recv, i):
        return pltpu.make_async_remote_copy(
            src_ref=src, dst_ref=dst, send_sem=sem_send, recv_sem=recv,
            device_id={"mem": peer_of(i, z, c)}, device_id_type=MESH,
        )

    def spread(send, got, sems):
        for i in (0, 1):
            remote(send.at[i], got.at[i], sems.at[0], i).start()

        def one(i, carry):
            j = mirror(i)
            remote(send.at[i], got.at[j], sems.at[j // 8], i).start()
            return carry

        lax.fori_loop(2, 30, one, 0)
        remote(send.at[30], got.at[30], sems.at[3], 30).start()

    def arrived(got, sems, g):
        size = 8 if g < 3 else 7
        view = got.at[pl.ds(8 * g, size)]
        pltpu.make_async_copy(view, view, sems.at[g]).wait()

    spread(send_p, got_p, sem_p)
    spread(send_low, got_low, sem_low)
    inv_centre = 1.0 / centre
    end_fetch(inn_hbm, inn, 1)

    def pack_rhs(i, carry):
        for slot in range(2):
            values = inn[blocks[2 * i + slot]]
            send_r[i, slot] = (values * inv_centre).astype(BF).reshape(3, 4, BLOCK)
        return carry

    lax.fori_loop(0, 32, pack_rhs, 0, unroll=2)
    spread(send_r, got_r, sem_r)
    own = [
        pltpu.make_async_copy(sent.at[31], got.at[31], sem_own.at[n])
        for n, (sent, got) in enumerate(
            ((send_p, got_p), (send_low, got_low), (send_r, got_r), (send_w, out_ref))
        )
    ]
    for copy in own[:3]:
        copy.start()
    for fetch in fetches:
        fetch.wait()
    for n in range(2):
        tile = taper_ref[n].astype(F32)
        turned = tile.T
        sym[n] = 0.5 * (tile + turned)
        flip[n] = turned.astype(BF)


    def local_part(k, carry):
        var = var_ref[k]
        keep = rho1 + sig1 * (centre - var)
        factor = 1.0 + (1.0 + rho2 - sig2 * var) * keep + sig2 * (centre - var)
        base_ref[k] = (factor * inv_centre) * inn[k]
        return carry

    lax.fori_loop(0, BAND, local_part, 0)
    keep_base = pltpu.make_async_copy(base_ref, base_hbm, sem_own.at[6])
    keep_base.start()

    for g in range(GROUPS):
        arrived(got_p, sem_p, g)
        arrived(got_low, sem_low, g)
    own[0].wait()
    own[1].wait()
    lows = got_low[...].reshape(128, 256)
    row = lax.broadcasted_iota(jnp.int32, (M, M), 0)
    col = lax.broadcasted_iota(jnp.int32, (M, M), 1)
    spot = row % 12 == 0
    centring = jnp.where(row == col, 1.0, 0.0) - 1.0 / 32.0
    centring = jnp.where(spot & (col % 12 == 0), centring, 0.0).astype(BF)
    wide_row = lax.broadcasted_iota(jnp.int32, (M, 128), 0)
    wide_col = lax.broadcasted_iota(jnp.int32, (M, 128), 1)
    part_of = jnp.where(wide_row == 12 * (wide_col // 4), 1.0, 0.0) - 1.0 / 32.0
    is_mean = lax.broadcasted_iota(jnp.int32, (M, BLOCK), 0) % 12 == 0
    for slot in range(2):
        raw = got_p[:, slot].reshape(M, BLOCK)
        halves = []
        for half in range(2):
            use = (wide_row % 12 == 0) & (wide_col % 4 == 2 * slot + half)
            weight = jnp.where(use, part_of, 0.0).astype(BF)
            halves.append(jnp.dot(weight, lows, preferred_element_type=F32))
        centred = jnp.dot(centring, raw, preferred_element_type=F32)
        centred = (centred + jnp.concatenate(halves, axis=1)) * INV
        pert[slot] = jnp.where(is_mean, centred, raw.astype(F32)).astype(BF)

    def to_lat(src, dst, recv, other):
        return pltpu.make_async_remote_copy(
            src_ref=src, dst_ref=dst, send_sem=sem_lat, recv_sem=recv,
            device_id={"lat": other}, device_id_type=MESH,
        )

    def to_both(src, dst_down, dst_up, sem_down, sem_up):
        to_lat(src, dst_down, sem_down, upper).start()
        to_lat(src, dst_up, sem_up, lower).start()

    def landed(view, sem):
        pltpu.make_async_copy(view, view, sem).wait()

    to_both(pert.at[0], pert_down, pert_up, sem_pert.at[0], sem_pert.at[1])
    north_on = pick[6]
    south_on = pick[7]

    def build(dst, base, left, right, tiles, which, on):
        def chunk(r, carry):
            rows = pl.ds(pl.multiple_of(r * 128, 128), 128)
            prod = lax.dot_general(
                left[:, rows], right[...], (((0,), (0,)), ((), ())), preferred_element_type=F32
            )
            share = pick[which]
            tile = tiles[1, rows].astype(F32) * share + tiles[0, rows].astype(F32) * (1.0 - share)
            value = tile * prod
            if on is not None:
                value = value * on
            dst[pl.ds(pl.multiple_of(base + r * 128, 128), 128)] = value.astype(BF)
            return carry

        lax.fori_loop(0, 4, chunk, 0)

    here0, here1 = pert.at[0], pert.at[1]
    build(mat_a, 0, here0, here0, sym, 0, None)
    build(mat_a, 512, here1, here0, flip, 2, pick[5])
    build(mat_b, 0, here0, here1, taper_ref, 2, pick[5])
    build(mat_b, 512, here1, here1, sym, 1, None)
    landed(pert_up, sem_pert.at[1])
    landed(pert_down, sem_pert.at[0])
    build(mat_a, 1024, pert_up, here0, flip, 3, north_on)
    build(mat_a, 1536, pert_down, here0, taper_ref, 4, south_on)

    var = (var_ref[blocks[62]], var_ref[blocks[63]])
    keep_d = [rho1 + sig1 * (centre - v) for v in var]
    keep_y = [(1.0 + rho2 - sig2 * v) * sig1 + sig2 for v in var]

    def times(parts, mat):
        total = None
        for n, part in enumerate(parts):
            prod = jnp.dot(part, mat[pl.ds(512 * n, 512)], preferred_element_type=F32)
            total = prod if total is None else total + prod
        return total

    def stage_a(g):
        arrived(got_r, sem_r, g)
        if g == 3:
            own[2].wait()
        rows = pl.ds(8 * g, 8)
        to_both(
            got_r.at[rows, 0], dir0_down.at[rows], dir0_up.at[rows],
            sem_d0.at[g, 0], sem_d0.at[g, 1],
        )

    def stage_b(g):
        rows = pl.ds(8 * g, 8)
        landed(dir0_up.at[rows], sem_d0.at[g, 1])
        landed(dir0_down.at[rows], sem_d0.at[g, 0])
        mine = [got_r[rows, s].reshape(96, BLOCK) for s in range(2)]
        above = dir0_up[rows].reshape(96, BLOCK)
        below = dir0_down[rows].reshape(96, BLOCK)
        prods = (times((mine[0], mine[1], above, below), mat_a), times(mine, mat_b))
        for s in range(2):
            dir1[g, s] = (keep_d[s] * mine[s].astype(F32) - sig1 * prods[s]).astype(BF)
            kept[g, s] = keep_y[s] * prods[s]
        to_both(
            dir1.at[g, 0], dir1_down.at[g], dir1_up.at[g], sem_d1.at[g, 0], sem_d1.at[g, 1]
        )

    def stage_c(g):
        landed(dir1_up.at[g], sem_d1.at[g, 1])
        landed(dir1_down.at[g], sem_d1.at[g, 0])
        mine = [dir1[g, s] for s in range(2)]
        prods = (
            times((mine[0], mine[1], dir1_up[g], dir1_down[g]), mat_a), times(mine, mat_b)
        )
        for s in range(2):
            total = (kept[g, s] + sig2 * prods[s]).astype(BF)
            send_w[pl.ds(8 * g, 8), s] = total.reshape(8, 3, 4, BLOCK)
        for i in range(8 * g, 8 * g + 8):
            if i == 31:
                continue
            j = i if i < 2 or i == 30 else mirror(i)
            remote(send_w.at[i], out_ref.at[j], sem_w, i).start()

    stage_a(0)
    stage_a(1)
    stage_b(0)
    stage_a(2)
    stage_b(1)
    stage_c(0)
    stage_a(3)
    stage_b(2)
    stage_c(1)
    stage_b(3)
    stage_c(2)
    stage_c(3)
    own[3].start()
    own[3].wait()
    keep_base.wait()

    most = pl.ds(0, 31)
    landed(out_ref.at[most], sem_w)
    for sent in (send_p, send_low, send_r, send_w):
        pltpu.make_async_copy(sent.at[most], sent.at[most], sem_send).wait()
    for _ in range(2):
        pltpu.make_async_copy(pert.at[0], pert.at[0], sem_lat).wait()
        pltpu.make_async_copy(dir0_up, dir0_up, sem_lat).wait()
        pltpu.make_async_copy(dir1_up, dir1_up, sem_lat).wait()


def exchange(equivalents, innovations, variance, tapers, blocks, pick, low, high):
    chunk = (3, 4, BLOCK)
    dma = pltpu.SemaphoreType.DMA
    return pl.pallas_call(
        exchange_kernel,
        out_shape=(
            jax.ShapeDtypeStruct((32, 2) + chunk, BF),
            jax.ShapeDtypeStruct((BAND, 12, BLOCK), F32),
        ),
        in_specs=[HB, HB, HB, HB, SM, SM, SM, SM],
        out_specs=(HB, HB),
        scratch_shapes=[
            pltpu.VMEM((BAND, 12, BLOCK), F32),
            pltpu.VMEM((BAND, 12, BLOCK), F32),
            pltpu.VMEM((BAND, 12, BLOCK), F32),
            pltpu.VMEM((BAND, 1, BLOCK), F32),
            pltpu.VMEM((2, BLOCK, BLOCK), BF),
            pltpu.VMEM((32, 2) + chunk, BF),
            pltpu.VMEM((32, 4, 256), BF),
            pltpu.VMEM((32, 2) + chunk, BF),
            pltpu.VMEM((32, 2) + chunk, BF),
            pltpu.VMEM((32, 4, 256), BF),
            pltpu.VMEM((32, 2) + chunk, BF),
            pltpu.VMEM((32, 2) + chunk, BF),
            pltpu.VMEM((2, M, BLOCK), BF),
            pltpu.VMEM((M, BLOCK), BF),
            pltpu.VMEM((M, BLOCK), BF),
            pltpu.VMEM((2, BLOCK, BLOCK), F32),
            pltpu.VMEM((2, BLOCK, BLOCK), BF),
            pltpu.VMEM((4 * BLOCK, BLOCK), BF),
            pltpu.VMEM((2 * BLOCK, BLOCK), BF),
            pltpu.VMEM((32,) + chunk, BF),
            pltpu.VMEM((32,) + chunk, BF),
            pltpu.VMEM((GROUPS, 2, 96, BLOCK), BF),
            pltpu.VMEM((GROUPS, 96, BLOCK), BF),
            pltpu.VMEM((GROUPS, 96, BLOCK), BF),
            pltpu.VMEM((GROUPS, 2, 96, BLOCK), F32),
            dma,
            dma((7,)),
            dma((2, BAND)),
            dma((GROUPS,)),
            dma((GROUPS,)),
            dma((GROUPS,)),
            dma,
            dma,
            dma((2,)),
            dma((GROUPS, 2)),
            dma((GROUPS, 2)),
        ],
        compiler_params=pltpu.CompilerParams(
            collective_id=0, has_side_effects=True, vmem_limit_bytes=LIMIT
        ),
        name="exchange",
    )(equivalents, innovations, variance, tapers, blocks, pick, low, high)


STEPS = 4
PER_STEP = BAND // STEPS


def finish_kernel(base_hbm, got_hbm, where, out_hbm, base, got, out, sem_base, sem_got, sem_out):
    bands = [pl.ds(step * PER_STEP, PER_STEP) for step in range(STEPS)]
    parts = [pl.ds(8 * n, 8) for n in range(4)]
    got_loads = [
        pltpu.make_async_copy(got_hbm.at[part], got.at[part], sem_got.at[n])
        for n, part in enumerate(parts)
    ]
    base_loads = [
        pltpu.make_async_copy(base_hbm.at[part], base.at[part], sem_base.at[n])
        for n, part in enumerate(bands)
    ]
    for load in got_loads + base_loads:
        load.start()
    for load in got_loads:
        load.wait()
    copies = []
    for step in range(STEPS):
        base_loads[step].wait()
        for n in range(step * PER_STEP, (step + 1) * PER_STEP):
            entry = where[n]
            change = got[entry // 2, entry % 2].reshape(12, BLOCK).astype(F32)
            out[:, pl.ds(n * BLOCK, BLOCK)] = base[n] - change
        cols = pl.ds(step * PER_STEP * BLOCK, PER_STEP * BLOCK)
        copies.append(
            pltpu.make_async_copy(out.at[:, cols], out_hbm.at[:, cols], sem_out.at[step])
        )
        copies[-1].start()
    for copy in copies:
        copy.wait()


def finish(base, got, where):
    dma = pltpu.SemaphoreType.DMA
    return pl.pallas_call(
        finish_kernel,
        out_shape=jax.ShapeDtypeStruct((12, BAND * BLOCK), F32),
        in_specs=[HB, HB, SM],
        out_specs=HB,
        scratch_shapes=[
            pltpu.VMEM((BAND, 12, BLOCK), F32),
            pltpu.VMEM((32, 2, 3, 4, BLOCK), BF),
            pltpu.VMEM((12, BAND * BLOCK), F32),
            dma((STEPS,)),
            dma((4,)),
            dma((STEPS,)),
        ],
        compiler_params=pltpu.CompilerParams(vmem_limit_bytes=LIMIT),
        name="finish",
    )(base, got, where)


def on_device(
    equivalents, innovations, obs_var, taper_tiles, region_blocks, pair_mask, taper_index,
    eig_low, eig_high,
):
    variance = obs_var.reshape(BAND, 1, BLOCK)
    blocks, pick, where = tables(
        jnp.transpose(taper_index, (2, 0, 1)), region_blocks, pair_mask
    )
    got, base = exchange(
        equivalents, innovations, variance, taper_tiles, blocks, pick, eig_low, eig_high
    )
    return finish(base, got, where)


def solution(mesh):
    return jax.shard_map(
        on_device,
        mesh=mesh,
        in_specs=(P("mem", "lat"), P("mem", "lat"), P("lat"), P(), P(), P(), P(), P(), P()),
        out_specs=P("mem", "lat"),
        check_vma=False,
    )
```

time: 141 us -> 136 us (0.965)
  Pallas kernels: 139 us -> 135 us
    pallas_call x3, Pallas kernels: 139 us -> 135 us  [the longest x1 129 us: exchange(): pl.pallas_call(exchange_kernel, out_shape=(jax.ShapeDtypeStruct((32, 2) +...]
where the time goes in v3:
time: 136 us
  Pallas kernels  135 us (99%)
    pallas_call x1, Pallas kernels, exchange(): pl.pallas_call(exchange_kernel, out_shape=(jax.ShapeDtypeStruct((32, 2) +...  129 us
    pallas_call x1, Pallas kernels, finish(): pl.pallas_call(finish_kernel, out_shape=jax.ShapeDtypeStruct((12, BAND *...  3.48 us

profile of v3, /device:TPU:1, one launch (start us, length us, event | category | flops | bytes accessed | tf_op | source)
XLA Modules:
  0.0 136.0 jit_solution(189406234759874289)
XLA Ops:
  1.3 2.6 %tables.1 = (s32[64]{0:T(128)}, f32[8]{0:T(128)}, s32[48]{0:T(128)}) custom-call(s32[3,16,48]{2,1,0:T(8,128)} %bitcast.3, s32[16,32]{1,0:T(8,128)} %region_ref.1, s32[16,48]{1,0:T(8,128)} %mask_ref.1), custom_call_target="tpu_custom_call" | custom-call | tf_op jit(solution)/shard_map/tables/pallas_call | solution.py:87
  3.9 128.7 %exchange.1 = (bf16[32,2,3,4,512]{4,3,2,1,0:T(4,128)(2,1)}, f32[48,12,512]{2,1,0:T(8,128)}) custom-call(f32[12,24576]{1,0:T(8,128)} %eq_hbm.1, f32[12,24576]{1,0:T(8,128)} %inn_hbm.1, f32[48,1,512]{2,1,0:T(1,128)} %bitcast.2, bf16[2,512,512]{2,1,0:T(8,128)(2,1)} %taper_hbm.1, s32[64]{0:T(128)} %get-tuple-element.10.blocks, f32[8]{0:T(128)} %get-tuple-element.11.pick, ...), custom_call_target="tpu_custom_call" | custom-call | tf_op jit(solution)/shard_map/exchange/pallas_call | solution.py:388
  132.6 3.5 %finish.1 = f32[12,24576]{1,0:T(8,128)} custom-call(f32[48,12,512]{2,1,0:T(8,128)} %get-tuple-element.12.base_hbm, bf16[32,2,3,4,512]{4,3,2,1,0:T(4,128)(2,1)} %get-tuple-element.13.got_hbm, s32[48]{0:T(128)} %get-tuple-element.14.where), custom_call_target="tpu_custom_call" | custom-call | tf_op jit(solution)/shard_map/finish/pallas_call | solution.py:478

commit v4 on v3

--- a/solution.py
+++ b/solution.py
@@ -168,7 +168,7 @@
         send_low[i] = jnp.concatenate(lows, axis=0).astype(BF)
         return carry
 
-    lax.fori_loop(0, 32, pack_pert, 0, unroll=2)
+    lax.fori_loop(0, 8, pack_pert, 0, unroll=2)
     pl.semaphore_wait(barrier, 33)
 
     def remote(src, dst, recv, i):
@@ -177,24 +177,29 @@
             device_id={"mem": peer_of(i, z, c)}, device_id_type=MESH,
         )
 
-    def spread(send, got, sems):
-        for i in (0, 1):
-            remote(send.at[i], got.at[i], sems.at[0], i).start()
+    def spread(send, got, sems, low=0, high=32):
+        if low == 0:
+            for i in (0, 1):
+                remote(send.at[i], got.at[i], sems.at[0], i).start()
 
         def one(i, carry):
             j = mirror(i)
             remote(send.at[i], got.at[j], sems.at[j // 8], i).start()
             return carry
 
-        lax.fori_loop(2, 30, one, 0)
-        remote(send.at[30], got.at[30], sems.at[3], 30).start()
+        lax.fori_loop(max(low, 2), min(high, 30), one, 0)
+        if high == 32:
+            remote(send.at[30], got.at[30], sems.at[3], 30).start()
 
     def arrived(got, sems, g):
         size = 8 if g < 3 else 7
         view = got.at[pl.ds(8 * g, size)]
         pltpu.make_async_copy(view, view, sems.at[g]).wait()
 
-    spread(send_p, got_p, sem_p)
+    spread(send_p, got_p, sem_p, 0, 8)
+    for g in range(1, GROUPS):
+        lax.fori_loop(8 * g, 8 * g + 8, pack_pert, 0, unroll=2)
+        spread(send_p, got_p, sem_p, 8 * g, 8 * g + 8)
     spread(send_low, got_low, sem_low)
     inv_centre = 1.0 / centre
     end_fetch(inn_hbm, inn, 1)
@@ -356,18 +361,13 @@
             j = i if i < 2 or i == 30 else mirror(i)
             remote(send_w.at[i], out_ref.at[j], sem_w, i).start()
 
-    stage_a(0)
-    stage_a(1)
-    stage_b(0)
-    stage_a(2)
-    stage_b(1)
-    stage_c(0)
-    stage_a(3)
-    stage_b(2)
-    stage_c(1)
-    stage_b(3)
-    stage_c(2)
-    stage_c(3)
+    for g in (0, 1):
+        stage_a(g)
+        stage_b(g)
+        stage_c(g)
+    for stage in (stage_a, stage_b, stage_c):
+        stage(2)
+        stage(3)
     own[3].start()
     own[3].wait()
     keep_base.wait()
@@ -438,7 +438,7 @@
     )(equivalents, innovations, variance, tapers, blocks, pick, low, high)
 
 
-STEPS = 4
+STEPS = 6
 PER_STEP = BAND // STEPS
 
 

time: 136 us -> 134 us (0.985)
  Pallas kernels: 135 us -> 132 us
    pallas_call x1, Pallas kernels: 129 us -> 126 us  [exchange(): pl.pallas_call(exchange_kernel, out_shape=(jax.ShapeDtypeStruct((32, 2) +...]
where the time goes in v4:
time: 134 us; the launch traced here: 133 us
  Pallas kernels  132 us (99%)
    pallas_call x1, Pallas kernels, exchange(): pl.pallas_call(exchange_kernel, out_shape=(jax.ShapeDtypeStruct((32, 2) +...  126 us
    pallas_call x1, Pallas kernels, finish(): pl.pallas_call(finish_kernel, out_shape=jax.ShapeDtypeStruct((12, BAND *...  3.48 us

profile of v4, /device:TPU:1, one launch (start us, length us, event | category | flops | bytes accessed | tf_op | source)
XLA Modules:
  0.0 133.5 jit_solution(4892744507998944310)
XLA Ops:
  1.3 2.6 %tables.1 = (s32[64]{0:T(128)}, f32[8]{0:T(128)}, s32[48]{0:T(128)}) custom-call(s32[3,16,48]{2,1,0:T(8,128)} %bitcast.3, s32[16,32]{1,0:T(8,128)} %region_ref.1, s32[16,48]{1,0:T(8,128)} %mask_ref.1), custom_call_target="tpu_custom_call" | custom-call | tf_op jit(solution)/shard_map/tables/pallas_call | solution.py:87
  3.9 126.1 %exchange.1 = (bf16[32,2,3,4,512]{4,3,2,1,0:T(4,128)(2,1)}, f32[48,12,512]{2,1,0:T(8,128)}) custom-call(f32[12,24576]{1,0:T(8,128)} %eq_hbm.1, f32[12,24576]{1,0:T(8,128)} %inn_hbm.1, f32[48,1,512]{2,1,0:T(1,128)} %bitcast.2, bf16[2,512,512]{2,1,0:T(8,128)(2,1)} %taper_hbm.1, s32[64]{0:T(128)} %get-tuple-element.10.blocks, f32[8]{0:T(128)} %get-tuple-element.11.pick, ...), custom_call_target="tpu_custom_call" | custom-call | tf_op jit(solution)/shard_map/exchange/pallas_call | solution.py:388
  130.0 3.5 %finish.1 = f32[12,24576]{1,0:T(8,128)} custom-call(f32[48,12,512]{2,1,0:T(8,128)} %get-tuple-element.12.base_hbm, bf16[32,2,3,4,512]{4,3,2,1,0:T(4,128)(2,1)} %get-tuple-element.13.got_hbm, s32[48]{0:T(128)} %get-tuple-element.14.where), custom_call_target="tpu_custom_call" | custom-call | tf_op jit(solution)/shard_map/finish/pallas_call | solution.py:478

commit v5 on v4

--- a/solution.py
+++ b/solution.py
@@ -46,61 +46,10 @@
 ROOT = 12.0**0.5
 
 
-def tables_kernel(index_ref, region_ref, mask_ref, blocks, pick, where, starts, low_starts):
-    me = lax.axis_index("mem")
-    z, c = me // 2, me % 2
-    band = lax.axis_index("lat")
-    lower = (band + 15) % 16
-
-    def scan(m, totals):
-        total, low_total = totals
-        starts[m] = total
-        low_starts[m] = low_total
-        dz = (m // 2 - z + 16) % 16
-        t = jnp.where(dz < 8, 15 - 2 * dz, 2 * dz - 16)
-        place = 2 * (2 * t + 1 - (m + c) % 2)
-        follow = jnp.minimum(total + 1, BAND - 1)
-        where[follow] = place + 1
-        where[total] = place
-        blocks[place] = total
-        blocks[place + 1] = follow
-        return total + region_ref[band, m], low_total + region_ref[lower, m]
-
-    lax.fori_loop(0, 32, scan, (jnp.int32(0), jnp.int32(0)), unroll=4)
-    start = starts[me]
-    second = jnp.minimum(start + 1, BAND - 1)
-
-    def one(on):
-        return jnp.where(on, 1.0, 0.0).astype(F32)
-
-    pick[0] = one(index_ref[0, band, start] == 1)
-    pick[1] = one(index_ref[0, band, second] == 1)
-    pick[2] = one(index_ref[1, band, start] == 1)
-    pick[3] = one(index_ref[2, band, start] == 1)
-    pick[4] = one(index_ref[2, lower, low_starts[me]] == 1)
-    pick[5] = one((region_ref[band, me] > 1) & (mask_ref[band, start] == 1))
-    pick[6] = one(band < 15)
-    pick[7] = one(band > 0)
-
-
-def tables(index, regions, mask):
-    return pl.pallas_call(
-        tables_kernel,
-        out_shape=(
-            jax.ShapeDtypeStruct((64,), jnp.int32),
-            jax.ShapeDtypeStruct((8,), F32),
-            jax.ShapeDtypeStruct((BAND,), jnp.int32),
-        ),
-        in_specs=[SM, SM, SM],
-        out_specs=(SM, SM, SM),
-        scratch_shapes=[pltpu.SMEM((32,), jnp.int32), pltpu.SMEM((32,), jnp.int32)],
-        name="tables",
-    )(index, regions, mask)
-
-
 def exchange_kernel(
-    eq_hbm, inn_hbm, var_hbm, taper_hbm, blocks, pick, lo_ref, hi_ref,
+    eq_hbm, inn_hbm, var_hbm, taper_hbm, index_ref, region_ref, mask_ref, lo_ref, hi_ref,
     out_ref, base_hbm,
+    starts, low_starts,
     base_ref,
     eq, inn, var_ref, taper_ref, send_p, send_low, send_r,
     got_p, got_low, got_r, send_w, pert, pert_up, pert_down, sym, flip, mat_a, mat_b,
@@ -152,13 +101,24 @@
     ]
     for fetch in fetches:
         fetch.start()
+    total = low_total = jnp.int32(0)
+    for m in range(32):
+        starts[m] = total
+        low_starts[m] = low_total
+        total = total + region_ref[band, m]
+        low_total = low_total + region_ref[lower, m]
+
+    def block_of(i, slot):
+        m = peer_of(i, z, c)
+        return starts[m] + slot * lax.div(region_ref[band, m], 2)
+
     top = lax.broadcasted_iota(jnp.int32, (12, BLOCK), 0) == 0
     end_fetch(eq_hbm, eq, 0)
 
     def pack_pert(i, carry):
         lows = []
         for slot in range(2):
-            values = eq[blocks[2 * i + slot]]
+            values = eq[block_of(i, slot)]
             total = jnp.sum(values, axis=0, keepdims=True) * (1.0 / ROOT)
             shift = (total - values[0:1]) * (1.0 / (ROOT - 1.0))
             mixed = jnp.where(top, total, (values - shift) * INV).astype(BF)
@@ -206,7 +166,7 @@
 
     def pack_rhs(i, carry):
         for slot in range(2):
-            values = inn[blocks[2 * i + slot]]
+            values = inn[block_of(i, slot)]
             send_r[i, slot] = (values * inv_centre).astype(BF).reshape(3, 4, BLOCK)
         return carry
 
@@ -280,8 +240,19 @@
         pltpu.make_async_copy(view, view, sem).wait()
 
     to_both(pert.at[0], pert_down, pert_up, sem_pert.at[0], sem_pert.at[1])
-    north_on = pick[6]
-    south_on = pick[7]
+    north_on = jnp.where(band < 15, 1.0, 0.0).astype(F32)
+    south_on = jnp.where(band > 0, 1.0, 0.0).astype(F32)
+    start = starts[me]
+    double = lax.div(region_ref[band, me], 2)
+    second = start + double
+    east_on = (double * mask_ref[band, start]).astype(F32)
+    picks = [
+        index_ref[kind, row, block].astype(F32)
+        for kind, row, block in (
+            (0, band, start), (0, band, second), (1, band, start), (2, band, start),
+            (2, lower, low_starts[me]),
+        )
+    ]
 
     def build(dst, base, left, right, tiles, which, on):
         def chunk(r, carry):
@@ -289,7 +260,7 @@
             prod = lax.dot_general(
                 left[:, rows], right[...], (((0,), (0,)), ((), ())), preferred_element_type=F32
             )
-            share = pick[which]
+            share = picks[which]
             tile = tiles[1, rows].astype(F32) * share + tiles[0, rows].astype(F32) * (1.0 - share)
             value = tile * prod
             if on is not None:
@@ -301,15 +272,15 @@
 
     here0, here1 = pert.at[0], pert.at[1]
     build(mat_a, 0, here0, here0, sym, 0, None)
-    build(mat_a, 512, here1, here0, flip, 2, pick[5])
-    build(mat_b, 0, here0, here1, taper_ref, 2, pick[5])
+    build(mat_a, 512, here1, here0, flip, 2, east_on)
+    build(mat_b, 0, here0, here1, taper_ref, 2, east_on)
     build(mat_b, 512, here1, here1, sym, 1, None)
     landed(pert_up, sem_pert.at[1])
     landed(pert_down, sem_pert.at[0])
     build(mat_a, 1024, pert_up, here0, flip, 3, north_on)
     build(mat_a, 1536, pert_down, here0, taper_ref, 4, south_on)
 
-    var = (var_ref[blocks[62]], var_ref[blocks[63]])
+    var = (var_ref[start], var_ref[second])
     keep_d = [rho1 + sig1 * (centre - v) for v in var]
     keep_y = [(1.0 + rho2 - sig2 * v) * sig1 + sig2 for v in var]
 
@@ -382,7 +353,7 @@
         pltpu.make_async_copy(dir1_up, dir1_up, sem_lat).wait()
 
 
-def exchange(equivalents, innovations, variance, tapers, blocks, pick, low, high):
+def exchange(equivalents, innovations, variance, tapers, index, regions, mask, low, high):
     chunk = (3, 4, BLOCK)
     dma = pltpu.SemaphoreType.DMA
     return pl.pallas_call(
@@ -391,9 +362,11 @@
             jax.ShapeDtypeStruct((32, 2) + chunk, BF),
             jax.ShapeDtypeStruct((BAND, 12, BLOCK), F32),
         ),
-        in_specs=[HB, HB, HB, HB, SM, SM, SM, SM],
+        in_specs=[HB, HB, HB, HB, SM, SM, SM, SM, SM],
         out_specs=(HB, HB),
         scratch_shapes=[
+            pltpu.SMEM((32,), jnp.int32),
+            pltpu.SMEM((32,), jnp.int32),
             pltpu.VMEM((BAND, 12, BLOCK), F32),
             pltpu.VMEM((BAND, 12, BLOCK), F32),
             pltpu.VMEM((BAND, 12, BLOCK), F32),
@@ -435,14 +408,16 @@
             collective_id=0, has_side_effects=True, vmem_limit_bytes=LIMIT
         ),
         name="exchange",
-    )(equivalents, innovations, variance, tapers, blocks, pick, low, high)
+    )(equivalents, innovations, variance, tapers, index, regions, mask, low, high)
 
 
 STEPS = 6
 PER_STEP = BAND // STEPS
 
 
-def finish_kernel(base_hbm, got_hbm, where, out_hbm, base, got, out, sem_base, sem_got, sem_out):
+def finish_kernel(
+    base_hbm, got_hbm, region_ref, out_hbm, base, got, out, where, sem_base, sem_got, sem_out
+):
     bands = [pl.ds(step * PER_STEP, PER_STEP) for step in range(STEPS)]
     parts = [pl.ds(8 * n, 8) for n in range(4)]
     got_loads = [
@@ -455,6 +430,19 @@
     ]
     for load in got_loads + base_loads:
         load.start()
+    me = lax.axis_index("mem")
+    z, c = me // 2, me % 2
+    band = lax.axis_index("lat")
+
+    def scan(m, total):
+        dz = (m // 2 - z + 16) % 16
+        t = jnp.where(dz < 8, 15 - 2 * dz, 2 * dz - 16)
+        place = 2 * (2 * t + 1 - (m + c) % 2)
+        where[jnp.minimum(total + 1, BAND - 1)] = place + 1
+        where[total] = place
+        return total + region_ref[band, m]
+
+    lax.fori_loop(0, 32, scan, jnp.int32(0), unroll=4)
     for load in got_loads:
         load.wait()
     copies = []
@@ -473,7 +461,7 @@
         copy.wait()
 
 
-def finish(base, got, where):
+def finish(base, got, regions):
     dma = pltpu.SemaphoreType.DMA
     return pl.pallas_call(
         finish_kernel,
@@ -484,13 +472,14 @@
             pltpu.VMEM((BAND, 12, BLOCK), F32),
             pltpu.VMEM((32, 2, 3, 4, BLOCK), BF),
             pltpu.VMEM((12, BAND * BLOCK), F32),
+            pltpu.SMEM((BAND,), jnp.int32),
             dma((STEPS,)),
             dma((4,)),
             dma((STEPS,)),
         ],
         compiler_params=pltpu.CompilerParams(vmem_limit_bytes=LIMIT),
         name="finish",
-    )(base, got, where)
+    )(base, got, regions)
 
 
 def on_device(
@@ -498,13 +487,11 @@
     eig_low, eig_high,
 ):
     variance = obs_var.reshape(BAND, 1, BLOCK)
-    blocks, pick, where = tables(
-        jnp.transpose(taper_index, (2, 0, 1)), region_blocks, pair_mask
+    got, base = exchange(
+        equivalents, innovations, variance, taper_tiles, jnp.transpose(taper_index, (2, 0, 1)),
+        region_blocks, pair_mask, eig_low, eig_high,
     )
-    got, base = exchange(
-        equivalents, innovations, variance, taper_tiles, blocks, pick, eig_low, eig_high
-    )
-    return finish(base, got, where)
+    return finish(base, got, region_blocks)
 
 
 def solution(mesh):

time: 134 us -> 132 us (0.985)
  Pallas kernels: 132 us -> 130 us
    pallas_call x1 -> x0, Pallas kernels: 2.57 us -> none  [tables(): pl.pallas_call(tables_kernel, out_shape=(jax.ShapeDtypeStruct((64,), jnp....]
where the time goes in v5:
time: 132 us
  Pallas kernels  130 us (98%)
    pallas_call x1, Pallas kernels, exchange(): pl.pallas_call(exchange_kernel, out_shape=(jax.ShapeDtypeStruct((32, 2) +...  127 us
    pallas_call x1, Pallas kernels, finish(): pl.pallas_call(finish_kernel, out_shape=jax.ShapeDtypeStruct((12, BAND *...  3.61 us

profile of v5, /device:TPU:1, one launch (start us, length us, event | category | flops | bytes accessed | tf_op | source)
XLA Modules:
  0.0 131.7 jit_solution(6261043109234470875)
XLA Ops:
  1.3 126.8 %exchange.1 = (bf16[32,2,3,4,512]{4,3,2,1,0:T(4,128)(2,1)}, f32[48,12,512]{2,1,0:T(8,128)}) custom-call(f32[12,24576]{1,0:T(8,128)} %eq_hbm.1, f32[12,24576]{1,0:T(8,128)} %inn_hbm.1, f32[48,1,512]{2,1,0:T(1,128)} %bitcast.2, bf16[2,512,512]{2,1,0:T(8,128)(2,1)} %taper_hbm.1, s32[3,16,48]{2,1,0:T(8,128)} %bitcast.3, s32[16,32]{1,0:T(8,128)} %region_ref.3, ...), custom_call_target="tpu_custom_call" | custom-call | tf_op jit(solution)/shard_map/exchange/pallas_call | solution.py:359
  128.1 3.6 %finish.1 = f32[12,24576]{1,0:T(8,128)} custom-call(f32[48,12,512]{2,1,0:T(8,128)} %get-tuple-element.7.base_hbm, bf16[32,2,3,4,512]{4,3,2,1,0:T(4,128)(2,1)} %get-tuple-element.8.got_hbm, s32[16,32]{1,0:T(8,128)} %region_ref.3), custom_call_target="tpu_custom_call" | custom-call | tf_op jit(solution)/shard_map/finish/pallas_call | solution.py:466

commit v6 on v5

--- a/solution.py
+++ b/solution.py
@@ -35,7 +35,7 @@
     t = i // 2
     odd = t % 2
     dz = (8 - (t + 1) // 2) * (2 * odd - 1)
-    return (z + dz + 16) % 16 * 2 + (c + 1 - i % 2) % 2
+    return lax.rem(z + dz + 16, 16) * 2 + lax.rem(c + 1 - i % 2, 2)
 
 
 def mirror(i):
@@ -84,23 +84,20 @@
 
     barrier = pltpu.get_barrier_semaphore()
 
-    def greet(i, carry):
-        pl.semaphore_signal(barrier, inc=1, device_id={"mem": peer_of(i, z, c)}, device_id_type=MESH)
-        return carry
-
-    lax.fori_loop(0, 31, greet, 0)
+    for i in range(31):
+        t = i // 2
+        dz = (8 - (t + 1) // 2) * (2 * (t % 2) - 1)
+        other = lax.rem(z + (dz + 16), 16) * 2 + (c if i % 2 else 1 - c)
+        pl.semaphore_signal(barrier, inc=1, device_id={"mem": other}, device_id_type=MESH)
     for other in (upper, lower):
         pl.semaphore_signal(barrier, inc=1, device_id={"lat": other}, device_id_type=MESH)
 
     centre, rho1, sig1, rho2, sig2 = coefficients(lo_ref[0], hi_ref[0])
     start_fetch(eq_hbm, eq, 0)
-    start_fetch(inn_hbm, inn, 1)
     fetches = [
         pltpu.make_async_copy(taper_hbm, taper_ref, sem_own.at[4]),
         pltpu.make_async_copy(var_hbm, var_ref, sem_own.at[5]),
     ]
-    for fetch in fetches:
-        fetch.start()
     total = low_total = jnp.int32(0)
     for m in range(32):
         starts[m] = total
@@ -157,6 +154,9 @@
         pltpu.make_async_copy(view, view, sems.at[g]).wait()
 
     spread(send_p, got_p, sem_p, 0, 8)
+    start_fetch(inn_hbm, inn, 1)
+    for fetch in fetches:
+        fetch.start()
     for g in range(1, GROUPS):
         lax.fori_loop(8 * g, 8 * g + 8, pack_pert, 0, unroll=2)
         spread(send_p, got_p, sem_p, 8 * g, 8 * g + 8)

time: 132 us -> 131 us (level)
  no operation moved by 1% of the time
where the time goes in v6:
time: 131 us
  Pallas kernels  130 us (99%)
    pallas_call x1, Pallas kernels, exchange(): pl.pallas_call(exchange_kernel, out_shape=(jax.ShapeDtypeStruct((32, 2) +...  126 us
    pallas_call x1, Pallas kernels, finish(): pl.pallas_call(finish_kernel, out_shape=jax.ShapeDtypeStruct((12, BAND *...  3.61 us

profile of v6, /device:TPU:1, one launch (start us, length us, event | category | flops | bytes accessed | tf_op | source)
XLA Modules:
  0.0 131.0 jit_solution(1324722041716087616)
XLA Ops:
  1.3 126.1 %exchange.1 = (bf16[32,2,3,4,512]{4,3,2,1,0:T(4,128)(2,1)}, f32[48,12,512]{2,1,0:T(8,128)}) custom-call(f32[12,24576]{1,0:T(8,128)} %eq_hbm.1, f32[12,24576]{1,0:T(8,128)} %inn_hbm.1, f32[48,1,512]{2,1,0:T(1,128)} %bitcast.2, bf16[2,512,512]{2,1,0:T(8,128)(2,1)} %taper_hbm.1, s32[3,16,48]{2,1,0:T(8,128)} %bitcast.3, s32[16,32]{1,0:T(8,128)} %region_ref.3, ...), custom_call_target="tpu_custom_call" | custom-call | tf_op jit(solution)/shard_map/exchange/pallas_call | solution.py:359
  127.4 3.6 %finish.1 = f32[12,24576]{1,0:T(8,128)} custom-call(f32[48,12,512]{2,1,0:T(8,128)} %get-tuple-element.7.base_hbm, bf16[32,2,3,4,512]{4,3,2,1,0:T(4,128)(2,1)} %get-tuple-element.8.got_hbm, s32[16,32]{1,0:T(8,128)} %region_ref.3), custom_call_target="tpu_custom_call" | custom-call | tf_op jit(solution)/shard_map/finish/pallas_call | solution.py:466
